TPU v7x, 128 devices: a whole 4x4x4 slice. The times are simulated.
128 devices in a mesh: grp: 2 (over z_lo), patch: 64 (over x, z_hi, y, core).
Axes of the slice: x: 4, y: 4, z: 4 (z_hi: 2, z_lo: 2; z = z_hi * 2 + z_lo), core: 2. Of those that a mesh axis runs over, the one named last changes fastest.
Arguments:
- displace: float32 [2, 131072, 384], P('grp', 'patch'), may hold values from -6 to 6
- velocity: float32 [2, 131072, 384], P('grp', 'patch'), may hold values from -6 to 6
- ext_force: float32 [2, 131072, 384], P('grp', 'patch'), may hold values from -6 to 6
- inv_mass: float32 [2, 131072, 128], P('grp', 'patch'), may hold values from 0.1 to 6
- thickness: float32 [2, 131072, 128], P('grp', 'patch'), may hold values from 0.5 to 2
- stiff_bands: bfloat16 [5, 384, 384], replicated, may hold values from -0.125 to 0.125
- pair_points: int32 [2, 64, 3, 1536], P('grp', 'patch'), may hold values from 0 to 6143
- pair_weights: float32 [2, 64, 3, 1536], P('grp', 'patch'), may hold values from 0.25 to 1
Outputs:
- displace_new: float32 [2, 131072, 384], P('grp', 'patch')
- velocity_new: float32 [2, 131072, 384], P('grp', 'patch')
Inputs may be any that keep to these rules, and one draw needn't show every extreme that they name: `pair_points`: entry e names the control point in row e // 3 of the sending block (rows counted within the block) and point e % 3 across the strip.
All inputs are finite; a program needn't handle non-finite values.
Results may differ from a plain program's by a relative error of at most 0.00094.
The roundings to bfloat16 on the way count: a program that leaves them out, or rounds other values in their place, can miss the bound.
Values may be sent and summed in bfloat16 or wider, within the bound.
No kernel may reach another device: no remote copies, remote signals or barrier semaphores. Data moves between devices by JAX's collectives and lax.ppermute only.
A program may use at most 192 MiB of HBM per device.

v0:
```python
import jax
import jax.numpy as jnp
from jax import lax
from jax.experimental import pallas as pl
from jax.experimental.pallas import tpu as pltpu
from jax.sharding import PartitionSpec as P

POINTS = 128
REACH = 2
SUBSTEPS = 4
EDGE = 3
COURANT = 0.4
ROWS = 2048
ROW = 384
SLOTS = 1536
HALO = 8
RUN = 129
PAIRS = 65
PLANE = 2080
TOP = 8
PAIR_ROWS = PAIRS * 16
BAND_ROWS = (PAIRS + 2) * 16
CHUNK = 208
F32 = jnp.float32
BF16 = jnp.bfloat16


def dot(a, b):
    return jnp.dot(a, b, preferred_element_type=F32)


def dot_nt(a, b):
    return lax.dot_general(a, b, (((1,), (1,)), ((), ())), preferred_element_type=F32)


def cols(c):
    return slice(c * 128, (c + 1) * 128)


def band_copies(stiff, wide_a, wide_b, wide_c, sem):
    copies = []
    for b in range(5):
        rows = pl.ds(b * ROW, ROW)
        next_rows = pl.ds((b + 1) * ROW, ROW)
        copies.append((stiff.at[b, :, pl.ds(0, 256)], wide_a.at[rows, :]))
        copies.append((stiff.at[b, :, pl.ds(256, 128)], wide_b.at[rows, pl.ds(0, 128)]))
        copies.append((stiff.at[b, :, pl.ds(0, 128)], wide_b.at[next_rows, pl.ds(128, 128)]))
        copies.append((stiff.at[b, :, pl.ds(128, 256)], wide_c.at[rows, :]))
    return [pltpu.make_async_copy(src, dst, sem.at[i]) for i, (src, dst) in enumerate(copies)]


def band_zeros(wide_b):
    wide_b[5 * ROW : 6 * ROW, 0:128] = jnp.zeros((ROW, 128), BF16)
    wide_b[0:ROW, 128:256] = jnp.zeros((ROW, 128), BF16)


def band_products(operand, start, wide_a, wide_b, wide_c):
    parts = [operand[i % 2, pl.ds(start + (i // 2) * 16, CHUNK), :] for i in range(6)]
    part_a = dot(jnp.concatenate(parts[:5], axis=1), wide_a[...])
    part_b = dot(jnp.concatenate(parts, axis=1), wide_b[...])
    part_c = dot(jnp.concatenate(parts[1:], axis=1), wide_c[...])
    even = [part_a[:, 0:128], part_a[:, 128:256], part_b[:, 0:128]]
    odd = [part_b[:, 128:256], part_c[:, 0:128], part_c[:, 128:256]]
    return even, odd


def plane_copies(array, halo_top, halo_bottom, plane, first, count, sem):
    copies = []
    for c in range(count):
        column = pl.ds(c * 128, 128)
        from_column = pl.ds(first + c * 128, 128)
        copies.append((array.at[0, :, column], plane.at[c, pl.ds(TOP + HALO, ROWS), :]))
        copies.append((halo_top.at[:, from_column], plane.at[c, pl.ds(TOP, HALO), :]))
        copies.append((halo_bottom.at[:, from_column], plane.at[c, pl.ds(TOP + HALO + ROWS, HALO), :]))
    return [pltpu.make_async_copy(src, dst, sem.at[i]) for i, (src, dst) in enumerate(copies)]


def clear_ends(plane, count):
    for c in range(count):
        plane[c, 0:TOP, :] = jnp.zeros((TOP, 128), F32)
        plane[c, PLANE - 8 : PLANE, :] = jnp.zeros((8, 128), F32)


def spread(k):
    return pl.ds(TOP + k, 16, stride=RUN)


def first_kernel(
    displace, velocity, thickness, stiff, halo_top, halo_bottom, points,
    force, compact, send_0, send_1, send_2,
    field, moving, thick, operand, force_vmem, wide_a, wide_b, wide_c, table,
    sem_field, sem_moving, sem_thick, sem_band, sem_out,
):
    field_in = plane_copies(displace, halo_top, halo_bottom, field, 0, 3, sem_field)
    moving_in = plane_copies(velocity, halo_top, halo_bottom, moving, 384, 3, sem_moving)
    thick_in = plane_copies(thickness, halo_top, halo_bottom, thick, 1280, 1, sem_thick)
    bands_in = band_copies(stiff, wide_a, wide_b, wide_c, sem_band)
    for copy in field_in + bands_in + moving_in + thick_in:
        copy.start()
    clear_ends(field, 3)
    clear_ends(moving, 3)
    clear_ends(thick, 1)
    band_zeros(wide_b)
    for copy in field_in:
        copy.wait()

    def make_operand(step, carry):
        for half in range(2):
            for c in range(3):
                operand[half, pl.ds(pl.multiple_of(step * 16, 16), 16), cols(c)] = field[
                    c, spread(2 * step + half - 2), :
                ].astype(BF16)
        return carry

    lax.fori_loop(0, PAIRS + 2, make_operand, 0)
    for copy in bands_in:
        copy.wait()
    force_out = []
    for chunk in range(PAIR_ROWS // CHUNK):
        start = chunk * CHUNK
        results = band_products(operand, start, wide_a, wide_b, wide_c)
        for half in range(2):
            for c in range(3):
                force_vmem[half, start : start + CHUNK, cols(c)] = results[half][c]
    for half in range(2):
        force_out.append(pltpu.make_async_copy(force_vmem.at[half], force.at[half], sem_out.at[half]))
    for copy in force_out:
        copy.start()
    for copy in moving_in + thick_in:
        copy.wait()
    lane = lax.broadcasted_iota(jnp.int32, (16, 128), 1)

    def make_compact(step, carry):
        for half in range(2):
            at = spread(2 * step + half)
            half_thick = 0.5 * thick[0, at, :]
            parts = [
                field[c, at, :]
                + 0.5 * moving[c, at, :]
                + half_thick * force_vmem[half, pl.ds(pl.multiple_of(step * 16, 16), 16), cols(c)]
                for c in range(3)
            ]
            compact[at, :] = jnp.where(
                lane < 3,
                parts[0],
                jnp.where(lane < 6, pltpu.roll(parts[1], 3, 1), pltpu.roll(parts[2], 6, 1)),
            )
        return carry

    lax.fori_loop(0, PAIRS, make_compact, 0)
    for group in range(16):
        start = TOP + HALO + group * 128
        turned = compact[start : start + 128, :].T[0:16, :]
        high = turned.astype(BF16)
        table[group * 16 : group * 16 + 16, 0:128] = high
        table[group * 16 : group * 16 + 16, 128:256] = (turned - high.astype(F32)).astype(BF16)
    place = lax.broadcasted_iota(jnp.int32, (128, SLOTS), 0)
    for j, send in enumerate([send_0, send_1, send_2]):
        entry = points[j : j + 1, :]
        row = (entry * 21846) >> 16
        point = entry - 3 * row
        low = row & 127
        group_of = row >> 7
        chosen = jnp.where(place == low, 1.0, 0.0).astype(BF16)
        picked = dot(table[...], jnp.concatenate([chosen, chosen], axis=0))
        total = jnp.zeros((16, SLOTS), F32)
        for group in range(16):
            total = total + jnp.where(group_of == group, picked[group * 16 : group * 16 + 16, :], 0.0)
        for c in range(3):
            value = jnp.where(
                point == 0,
                total[3 * c : 3 * c + 1, :],
                jnp.where(point == 1, total[3 * c + 1 : 3 * c + 2, :], total[3 * c + 2 : 3 * c + 3, :]),
            )
            send[c : c + 1, :] = value
    for copy in force_out:
        copy.wait()


def couple_kernel(where_am_i, got_0, got_1, got_2, points, weights, compact, coupling, edge_top, edge_bottom, total):
    block = where_am_i[1]
    blocks = where_am_i[2]
    place = lax.broadcasted_iota(jnp.int32, (128, SLOTS), 0)
    line = lax.broadcasted_iota(jnp.int32, (16, SLOTS), 0)
    summed = None
    for j, got in enumerate([got_0, got_1, got_2]):
        entry = points[j : j + 1, :]
        row = (entry * 21846) >> 16
        point = entry - 3 * row
        low = row & 127
        group_of = row >> 7
        neighbour = block + (j - 1)
        present = jnp.where((neighbour >= 0) & (neighbour < blocks), 1.0, 0.0)
        weight = weights[j : j + 1, :] * present
        spread_out = jnp.zeros((16, SLOTS), F32)
        for c in range(4):
            value = weight * got[c : c + 1, :] if c < 3 else weight
            spread_out = jnp.where(line == 3 * c + point, value, spread_out)
        high = spread_out.astype(BF16)
        rest = (spread_out - high.astype(F32)).astype(BF16)
        zero = jnp.zeros((16, SLOTS), BF16)
        right = jnp.concatenate(
            [jnp.where(group_of == group, high, zero) for group in range(16)]
            + [jnp.where(group_of == group, rest, zero) for group in range(16)],
            axis=0,
        )
        chosen = jnp.where(place == low, 1.0, 0.0).astype(BF16)
        part = dot_nt(chosen, right)
        summed = part if summed is None else summed + part
    total[...] = summed[:, 0:256] + summed[:, 256:512]
    lane = lax.broadcasted_iota(jnp.int32, (128, 128), 1)
    for group in range(16):
        half = total[:, (group // 8) * 128 : (group // 8) * 128 + 128]
        shift = (group % 8) * 16
        block_sum = pltpu.roll(half, 128 - shift, 1) if shift else half
        weight_sum = jnp.where(
            lane < 3,
            pltpu.roll(block_sum, 119, 1),
            jnp.where(lane < 6, pltpu.roll(block_sum, 122, 1), pltpu.roll(block_sum, 125, 1)),
        )
        start = TOP + HALO + group * 128
        here = block_sum - compact[start : start + 128, :] * weight_sum
        here = jnp.where(lane < 9, here, 0.0)
        coupling[group * 128 : group * 128 + 128, :] = here
        if group == 0:
            edge_top[...] = here[0:8, :]
        if group == 15:
            edge_bottom[...] = here[120:128, :]


def step_kernel(
    where_am_i, stiffest, displace, velocity, ext_force, inv_mass, thickness, stiff, halo_top, halo_bottom,
    force, coupling, couple_top, couple_bottom,
    new_field, new_moving,
    field, moving, outer, mass, thick, couple, force_vmem,
    state, speed, push, drag, operand_a, operand_b, wide_a, wide_b, wide_c,
    sem_field, sem_moving, sem_outer, sem_mass, sem_thick, sem_couple, sem_force, sem_band, sem_out,
):
    fine = where_am_i[0] == 1
    arrays = [
        plane_copies(displace, halo_top, halo_bottom, field, 0, 3, sem_field),
        plane_copies(velocity, halo_top, halo_bottom, moving, 384, 3, sem_moving),
        plane_copies(ext_force, halo_top, halo_bottom, outer, 768, 3, sem_outer),
        plane_copies(inv_mass, halo_top, halo_bottom, mass, 1152, 1, sem_mass),
        plane_copies(thickness, halo_top, halo_bottom, thick, 1280, 1, sem_thick),
    ]
    arrays.append(
        [
            pltpu.make_async_copy(coupling, couple.at[pl.ds(TOP + HALO, ROWS), :], sem_couple.at[0]),
            pltpu.make_async_copy(couple_top, couple.at[pl.ds(TOP, HALO), :], sem_couple.at[1]),
            pltpu.make_async_copy(couple_bottom, couple.at[pl.ds(TOP + HALO + ROWS, HALO), :], sem_couple.at[2]),
            pltpu.make_async_copy(force, force_vmem, sem_force.at[0]),
        ]
    )
    bands_in = band_copies(stiff, wide_a, wide_b, wide_c, sem_band)
    for group in arrays + [bands_in]:
        for copy in group:
            copy.start()
    clear_ends(field, 3)
    clear_ends(moving, 3)
    clear_ends(outer, 3)
    clear_ends(mass, 1)
    clear_ends(thick, 1)
    couple[PLANE - 8 : PLANE, :] = jnp.zeros((8, 128), F32)
    band_zeros(wide_b)
    limit = jnp.full((16, 128), stiffest[0], F32)
    base_step = COURANT * (1.0 / jnp.sqrt(limit))
    size = jnp.where(fine, base_step, SUBSTEPS * base_step)
    square = size * size
    for group in arrays:
        for copy in group:
            copy.wait()
    lane = lax.broadcasted_iota(jnp.int32, (16, 128), 1)

    def first_step(step, carry):
        for half in range(2):
            at = spread(2 * step + half)
            tile = pl.ds(pl.multiple_of(step * 16, 16), 16)
            next_tile = pl.ds(pl.multiple_of(step * 16 + 16, 16), 16)
            scaled = square * mass[0, at, :]
            pull = scaled * thick[0, at, :]
            drag[half, tile, :] = pull
            both = couple[at, :]
            for c in range(3):
                here = jnp.where(lane < 3, pltpu.roll(both, 128 - 3 * c, 1) if c else both, 0.0)
                drive = scaled * (outer[c, at, :] + here)
                push[half, tile, cols(c)] = drive
                new_speed = size * moving[c, at, :] + (drive - pull * force_vmem[half, tile, cols(c)])
                place = field[c, at, :] + new_speed
                speed[half, tile, cols(c)] = new_speed
                state[half, tile, cols(c)] = place
                operand_a[half, next_tile, cols(c)] = place.astype(BF16)
        return carry

    lax.fori_loop(0, PAIRS, first_step, 0)
    for copy in bands_in:
        copy.wait()

    def fill_ends(operand):
        for c in range(3):
            operand[0, 0:16, cols(c)] = pltpu.roll(state[1, 63 * 16 : 64 * 16, cols(c)], 1, 0).astype(BF16)
            operand[1, 0:16, cols(c)] = pltpu.roll(state[0, 64 * 16 : 65 * 16, cols(c)], 1, 0).astype(BF16)
            operand[0, 66 * 16 : 67 * 16, cols(c)] = pltpu.roll(state[1, 0:16, cols(c)], 15, 0).astype(BF16)
            operand[1, 66 * 16 : 67 * 16, cols(c)] = pltpu.roll(state[0, 16:32, cols(c)], 15, 0).astype(BF16)

    def substep(operand, following):
        def update(start, results):
            rows = slice(start, start + CHUNK)
            for half in range(2):
                pull = drag[half, rows, :]
                for c in range(3):
                    new_speed = speed[half, rows, cols(c)] + (push[half, rows, cols(c)] - pull * results[half][c])
                    place = state[half, rows, cols(c)] + new_speed
                    speed[half, rows, cols(c)] = new_speed
                    state[half, rows, cols(c)] = place
                    if following is not None:
                        following[half, start + 16 : start + 16 + CHUNK, cols(c)] = place.astype(BF16)

        before = None
        for chunk in range(PAIR_ROWS // CHUNK):
            start = chunk * CHUNK
            results = band_products(operand, start, wide_a, wide_b, wide_c)
            if before is not None:
                update(*before)
            before = (start, results)
        update(*before)

    @pl.when(fine)
    def _():
        fill_ends(operand_a)
        substep(operand_a, operand_b)
        fill_ends(operand_b)
        substep(operand_b, operand_a)
        fill_ends(operand_a)
        substep(operand_a, None)

    inverse = 1.0 / size

    def last(step, carry):
        for half in range(2):
            at = spread(2 * step + half)
            tile = pl.ds(pl.multiple_of(step * 16, 16), 16)
            for c in range(3):
                field[c, at, :] = state[half, tile, cols(c)]
                moving[c, at, :] = speed[half, tile, cols(c)] * inverse
        return carry

    lax.fori_loop(0, PAIRS, last, 0)
    out = []
    for c in range(3):
        inner = pl.ds(TOP + HALO, ROWS)
        out.append(pltpu.make_async_copy(field.at[c, inner, :], new_field.at[0, :, pl.ds(c * 128, 128)], sem_out.at[c]))
        out.append(
            pltpu.make_async_copy(moving.at[c, inner, :], new_moving.at[0, :, pl.ds(c * 128, 128)], sem_out.at[3 + c])
        )
    for copy in out:
        copy.start()
    for copy in out:
        copy.wait()


ANY = pl.BlockSpec(memory_space=pl.ANY)
IN_VMEM = pl.BlockSpec(memory_space=pltpu.VMEM)
IN_SMEM = pl.BlockSpec(memory_space=pltpu.SMEM)
DMA = pltpu.SemaphoreType.DMA


def shape(*dims):
    return jax.ShapeDtypeStruct(dims, F32)


def per_device(
    displace, velocity, ext_force, inv_mass, thickness, stiff_bands, pair_points, pair_weights
):
    group = lax.axis_index("grp")
    block = lax.axis_index("patch")
    blocks = lax.axis_size("patch")
    where_am_i = jnp.stack([group, block, jnp.int32(blocks)]).astype(jnp.int32)
    points = pair_points[0, 0]
    weights = pair_weights[0, 0]
    down = [(i, i + 1) for i in range(blocks - 1)]
    up = [(i + 1, i) for i in range(blocks - 1)]
    arrays = [displace, velocity, ext_force, inv_mass, thickness]
    first_rows = jnp.concatenate([a[0, :HALO] for a in arrays], axis=1)
    last_rows = jnp.concatenate([a[0, ROWS - HALO :] for a in arrays], axis=1)
    halo_top = lax.ppermute(last_rows, "patch", down)
    halo_bottom = lax.ppermute(first_rows, "patch", up)
    local = jnp.broadcast_to(jnp.max(inv_mass * thickness), (2 * blocks, 1, 128))
    stiffest = jnp.max(lax.all_to_all(local, ("grp", "patch"), 0, 0)).reshape(1)

    bands = [
        pltpu.VMEM((5 * ROW, 256), BF16),
        pltpu.VMEM((6 * ROW, 256), BF16),
        pltpu.VMEM((5 * ROW, 256), BF16),
    ]
    plane_3 = pltpu.VMEM((3, PLANE, 128), F32)
    plane_1 = pltpu.VMEM((1, PLANE, 128), F32)
    full = pltpu.VMEM((2, PAIR_ROWS, ROW), F32)
    band_operand = pltpu.VMEM((2, BAND_ROWS, ROW), BF16)
    force, compact, send_0, send_1, send_2 = pl.pallas_call(
        first_kernel,
        out_shape=(
            shape(2, PAIR_ROWS, ROW),
            shape(PLANE, 128),
            shape(3, SLOTS),
            shape(3, SLOTS),
            shape(3, SLOTS),
        ),
        in_specs=[ANY] * 6 + [IN_VMEM],
        out_specs=[ANY] + [IN_VMEM] * 4,
        scratch_shapes=[plane_3, plane_3, plane_1, band_operand, full]
        + bands
        + [pltpu.VMEM((256, 256), BF16)]
        + [DMA((9,)), DMA((9,)), DMA((3,)), DMA((20,)), DMA((2,))],
        name="first_force",
    )(displace, velocity, thickness, stiff_bands, halo_top, halo_bottom, points)

    both = ("grp", "patch")
    got = []
    sends = [send_0, send_1, send_2]
    for j in range(3):
        pairs = []
        for g in range(2):
            for p in range(blocks):
                target = p + 1 - j
                if 0 <= target < blocks:
                    pairs.append((g * blocks + p, (1 - g) * blocks + target))
        got.append(lax.ppermute(sends[2 - j], both, pairs))

    coupling, edge_top, edge_bottom = pl.pallas_call(
        couple_kernel,
        out_shape=(shape(ROWS, 128), shape(8, 128), shape(8, 128)),
        in_specs=[IN_SMEM] + [IN_VMEM] * 6,
        out_specs=[IN_VMEM] * 3,
        scratch_shapes=[pltpu.VMEM((128, 256), F32)],
        name="couple",
    )(where_am_i, *got, points, weights, compact)
    couple_top = lax.ppermute(edge_bottom, "patch", down)
    couple_bottom = lax.ppermute(edge_top, "patch", up)

    new_field, new_moving = pl.pallas_call(
        step_kernel,
        out_shape=(shape(1, ROWS, ROW), shape(1, ROWS, ROW)),
        in_specs=[IN_SMEM] * 2 + [ANY] * 12,
        out_specs=[ANY] * 2,
        scratch_shapes=[plane_3, plane_3, plane_3, plane_1, plane_1, pltpu.VMEM((PLANE, 128), F32), full]
        + [full, full, full, pltpu.VMEM((2, PAIR_ROWS, 128), F32)]
        + [band_operand, band_operand]
        + bands
        + [DMA((9,)), DMA((9,)), DMA((9,)), DMA((3,)), DMA((3,)), DMA((3,)), DMA((1,)), DMA((20,)), DMA((6,))],
        name="steps",
    )(
        where_am_i, stiffest, displace, velocity, ext_force, inv_mass, thickness, stiff_bands,
        halo_top, halo_bottom, force, coupling, couple_top, couple_bottom,
    )
    return new_field, new_moving


def solution(mesh):
    spec3 = P("grp", "patch", None)
    spec4 = P("grp", "patch", None, None)
    return jax.shard_map(
        per_device,
        mesh=mesh,
        in_specs=(spec3, spec3, spec3, spec3, spec3, P(), spec4, spec4),
        out_specs=(spec3, spec3),
        check_vma=False,
    )
```

profile of v0, /device:TPU:121, one launch (start us, length us, event | category | flops | bytes accessed | tf_op | source)
XLA Modules:
  0.0 106.8 jit_solution(12640391676124522878)
XLA Ops:
  0.6 0.7 constant_dynamic-update-slice_fusion.9
  1.4 0.7 constant_dynamic-update-slice_fusion.8
  2.1 0.7 constant_dynamic-update-slice_fusion.7
  2.8 0.7 constant_dynamic-update-slice_fusion.6
  3.5 0.7 constant_dynamic-update-slice_fusion.5
  4.2 2.6 %collective-permute-start.1 = (f32[8,1408]{1,0:T(8,128)S(1)}, f32[8,1408]{1,0:T(8,128)S(1)}, u32[]{:S(2)}, u32[]{:S(2)}) collective-permute-start(f32[8,1408]{1,0:T(8,128)S(1)} %get-tuple-element.24), channel_id=1, source_target_pairs={{1,0},{2,1},{3,2},{4,3},{5,4},{6,5},{7,6},{8,7},{9,8},{10,9},{11,1... | collective-permute-start | bytes 135176 | tf_op jit(solution)/shard_map/ppermute | solution.py:387
  6.8 7.5 %collective-permute-start = (f32[8,1408]{1,0:T(8,128)S(1)}, f32[8,1408]{1,0:T(8,128)S(1)}, u32[]{:S(2)}, u32[]{:S(2)}) collective-permute-start(f32[8,1408]{1,0:T(8,128)S(1)} %get-tuple-element.25), channel_id=1, source_target_pairs={{0,1},{1,2},{2,3},{3,4},{4,5},{5,6},{6,7},{7,8},{8,9},{9,10},{10,1... | collective-permute-start | bytes 135176 | tf_op jit(solution)/shard_map/ppermute | solution.py:386
  14.3 2.4 %multiply_reduce_fusion = f32[]{:T(128)} fusion(f32[1,2048,128]{2,1,0:T(8,128)} %inv_mass.1, f32[1,2048,128]{2,1,0:T(8,128)} %thickness.3), kind=kLoop, calls=%fused_computation | loop fusion | flops 524287 | bytes 2097156 | tf_op jit(solution)/shard_map/reduce_max | solution.py:388
  16.7 1.3 %broadcast_in_dim.3 = f32[128,1,128]{2,1,0:T(1,128)} broadcast(f32[]{:T(128)} %multiply_reduce_fusion), dimensions={} | broadcast | bytes 65540 | tf_op jit(solution)/shard_map/broadcast_in_dim | solution.py:388
  18.0 9.3 %all-to-all-start = ((f32[128,1,128]{2,1,0:T(1,128)}), f32[128,1,128]{2,1,0:T(1,128)S(1)}, u32[]{:S(2)}, u32[]{:S(2)}) async-start(f32[128,1,128]{2,1,0:T(1,128)} %broadcast_in_dim.3), calls=%async_computation | async-start | bytes 131072 | tf_op jit(solution)/shard_map/all_to_all | solution.py:389
  27.3 1.3 %copy.16 = s32[1,1,3,1536]{3,2,1,0:T(4,128)} copy(s32[1,1,3,1536]{3,1,2,0:T(1,128)} %param.14) | data formatting | bytes 36864
  29.3 17.2 %first_force.1 = (f32[2,1040,384]{2,1,0:T(8,128)}, f32[2080,128]{1,0:T(8,128)}, f32[3,1536]{1,0:T(4,128)}, f32[3,1536]{1,0:T(4,128)}, f32[3,1536]{1,0:T(4,128)}) custom-call(f32[1,2048,384]{2,1,0:T(8,128)} %displace.3, f32[1,2048,384]{2,1,0:T(8,128)} %velocity.3, f32[1,2048,128]{2,1,0:T(8,128)} %thickness.3, bf16[5,384,384]{2,1,0:T(8,128)(2,1)} %stiff.3, ...), custom_call_target="tpu_custom_call" | custom-call | tf_op jit(solution)/shard_map/first_force/pallas_call | solution.py:400
  46.5 2.5 %collective-permute-start.2 = (f32[3,1536]{1,0:T(4,128)}, f32[3,1536]{1,0:T(4,128)S(1)}, u32[]{:S(2)}, u32[]{:S(2)}) collective-permute-start(f32[3,1536]{1,0:T(4,128)} %get-tuple-element.11), channel_id=1, source_target_pairs={{0,65},{1,66},{2,67},{3,68},{4,69},{5,70},{6,71},{7,72},{8,73},{9,... | collective-permute-start | bytes 55304 | tf_op jit(solution)/shard_map/ppermute | solution.py:428
  49.0 0.8 collective-permute-start.3
  49.8 3.0 %collective-permute-start.4 = (f32[3,1536]{1,0:T(4,128)}, f32[3,1536]{1,0:T(4,128)S(1)}, u32[]{:S(2)}, u32[]{:S(2)}) collective-permute-start(f32[3,1536]{1,0:T(4,128)} %get-tuple-element.13), channel_id=1, source_target_pairs={{1,64},{2,65},{3,66},{4,67},{5,68},{6,69},{7,70},{8,71},{9,72},{10... | collective-permute-start | bytes 55304 | tf_op jit(solution)/shard_map/ppermute | solution.py:428
  52.7 0.7 pad_add_fusion.where_am_i
  53.4 0.6 copy.15
  54.0 5.3 %collective-permute-done.4.got_2 = f32[3,1536]{1,0:T(4,128)S(1)} collective-permute-done((f32[3,1536]{1,0:T(4,128)}, f32[3,1536]{1,0:T(4,128)S(1)}, u32[]{:S(2)}, u32[]{:S(2)}) %collective-permute-start.4) | collective-permute-done | bytes 18464 | tf_op jit(solution)/shard_map/ppermute | solution.py:428
  59.9 5.3 %couple.1 = (f32[2048,128]{1,0:T(8,128)}, f32[8,128]{1,0:T(8,128)}, f32[8,128]{1,0:T(8,128)}) custom-call(s32[3]{0:T(128)} %pad_add_fusion.where_am_i, f32[3,1536]{1,0:T(4,128)} %copy-done.2, f32[3,1536]{1,0:T(4,128)} %copy-done.3, f32[3,1536]{1,0:T(4,128)} %copy-done.4, s32[3,1536]{1,0:T(4,128)} %bitcast.32, f32[3,1536]{1,0:T(4,128)} %bitcast.33, ...), custom_call_target="tpu_custom_call" | custom-call | tf_op jit(solution)/shard_map/couple/pallas_call | solution.py:430
  65.2 1.9 %collective-permute-start.5 = (f32[8,128]{1,0:T(8,128)}, f32[8,128]{1,0:T(8,128)S(1)}, u32[]{:S(2)}, u32[]{:S(2)}) collective-permute-start(f32[8,128]{1,0:T(8,128)} %get-tuple-element.16), channel_id=1, source_target_pairs={{0,1},{1,2},{2,3},{3,4},{4,5},{5,6},{6,7},{7,8},{8,9},{9,10},{10,1... | collective-permute-start | bytes 12296 | tf_op jit(solution)/shard_map/ppermute | solution.py:438
  67.1 2.4 %collective-permute-start.6 = (f32[8,128]{1,0:T(8,128)}, f32[8,128]{1,0:T(8,128)S(1)}, u32[]{:S(2)}, u32[]{:S(2)}) collective-permute-start(f32[8,128]{1,0:T(8,128)} %get-tuple-element.17), channel_id=1, source_target_pairs={{1,0},{2,1},{3,2},{4,3},{5,4},{6,5},{7,6},{8,7},{9,8},{10,9},{11,1... | collective-permute-start | bytes 12296 | tf_op jit(solution)/shard_map/ppermute | solution.py:439
  69.5 0.7 reduce_max.19
  70.2 6.5 %collective-permute-done.6.couple_bottom = f32[8,128]{1,0:T(8,128)S(1)} collective-permute-done((f32[8,128]{1,0:T(8,128)}, f32[8,128]{1,0:T(8,128)S(1)}, u32[]{:S(2)}, u32[]{:S(2)}) %collective-permute-start.6) | collective-permute-done | bytes 4128 | tf_op jit(solution)/shard_map/ppermute | solution.py:439
  77.4 29.3 %steps.1 = (f32[1,2048,384]{2,1,0:T(8,128)}, f32[1,2048,384]{2,1,0:T(8,128)}) custom-call(s32[3]{0:T(128)} %pad_add_fusion.where_am_i, f32[1]{0:T(128)} %bitcast.3.stiffest, f32[1,2048,384]{2,1,0:T(8,128)} %displace.3, f32[1,2048,384]{2,1,0:T(8,128)} %velocity.3, f32[1,2048,384]{2,1,0:T(8,128)} %ext_force.1, f32[1,2048,128]{2,1,0:T(8,128)} %inv_mass.1, ...), custom_call_target="tpu_custom_call" | custom-call | tf_op jit(solution)/shard_map/steps/pallas_call | solution.py:441
  (22 shorter events, 1.8 us)
Async XLA Ops:
  4.2 24.4 %collective-permute-start.1 = (f32[8,1408]{1,0:T(8,128)S(1)}, f32[8,1408]{1,0:T(8,128)S(1)}, u32[]{:S(2)}, u32[]{:S(2)}) collective-permute-start(f32[8,1408]{1,0:T(8,128)S(1)} %get-tuple-element.24), channel_id=1, source_target_pairs={{1,0},{2,1},{3,2},{4,3},{5,4},{6,5},{7,6},{8,7},{9,8},{10,9},{11,1... | collective-permute-start | bytes 135176 | tf_op jit(solution)/shard_map/ppermute | solution.py:387
  6.8 21.9 %collective-permute-start = (f32[8,1408]{1,0:T(8,128)S(1)}, f32[8,1408]{1,0:T(8,128)S(1)}, u32[]{:S(2)}, u32[]{:S(2)}) collective-permute-start(f32[8,1408]{1,0:T(8,128)S(1)} %get-tuple-element.25), channel_id=1, source_target_pairs={{0,1},{1,2},{2,3},{3,4},{4,5},{5,6},{6,7},{7,8},{8,9},{9,10},{10,1... | collective-permute-start | bytes 135176 | tf_op jit(solution)/shard_map/ppermute | solution.py:386
  18.0 51.5 %all-to-all-start = ((f32[128,1,128]{2,1,0:T(1,128)}), f32[128,1,128]{2,1,0:T(1,128)S(1)}, u32[]{:S(2)}, u32[]{:S(2)}) async-start(f32[128,1,128]{2,1,0:T(1,128)} %broadcast_in_dim.3), calls=%async_computation | async-start | bytes 131072 | tf_op jit(solution)/shard_map/all_to_all | solution.py:389
  28.7 0.6 copy-start
  28.7 0.6 copy-start.1
  29.3 24.1 %copy-start.5 = (f32[1,1,3,1536]{3,1,2,0:T(1,128)S(1)}, f32[1,1,3,1536]{3,1,2,0:T(1,128)}, u32[]{:S(2)}) copy-start(f32[1,1,3,1536]{3,1,2,0:T(1,128)} %param.15) | copy-start | bytes 55300
  46.5 7.5 %collective-permute-start.2 = (f32[3,1536]{1,0:T(4,128)}, f32[3,1536]{1,0:T(4,128)S(1)}, u32[]{:S(2)}, u32[]{:S(2)}) collective-permute-start(f32[3,1536]{1,0:T(4,128)} %get-tuple-element.11), channel_id=1, source_target_pairs={{0,65},{1,66},{2,67},{3,68},{4,69},{5,70},{6,71},{7,72},{8,73},{9,... | collective-permute-start | bytes 55304 | tf_op jit(solution)/shard_map/ppermute | solution.py:428
  49.0 5.0 %collective-permute-start.3 = (f32[3,1536]{1,0:T(4,128)}, f32[3,1536]{1,0:T(4,128)S(1)}, u32[]{:S(2)}, u32[]{:S(2)}) collective-permute-start(f32[3,1536]{1,0:T(4,128)} %get-tuple-element.12), channel_id=1, source_target_pairs={{0,64},{1,65},{2,66},{3,67},{4,68},{5,69},{6,70},{7,71},{8,72},{9,... | collective-permute-start | bytes 55304 | tf_op jit(solution)/shard_map/ppermute | solution.py:428
  49.8 9.6 %collective-permute-start.4 = (f32[3,1536]{1,0:T(4,128)}, f32[3,1536]{1,0:T(4,128)S(1)}, u32[]{:S(2)}, u32[]{:S(2)}) collective-permute-start(f32[3,1536]{1,0:T(4,128)} %get-tuple-element.13), channel_id=1, source_target_pairs={{1,64},{2,65},{3,66},{4,67},{5,68},{6,69},{7,70},{8,71},{9,72},{10... | collective-permute-start | bytes 55304 | tf_op jit(solution)/shard_map/ppermute | solution.py:428
  54.0 5.3 %copy-start.2 = (f32[3,1536]{1,0:T(4,128)}, f32[3,1536]{1,0:T(4,128)S(1)}, u32[]{:S(2)}) copy-start(f32[3,1536]{1,0:T(4,128)S(1)} %collective-permute-done.2.got_0) | copy-start | bytes 55300
  54.0 5.3 %copy-start.3 = (f32[3,1536]{1,0:T(4,128)}, f32[3,1536]{1,0:T(4,128)S(1)}, u32[]{:S(2)}) copy-start(f32[3,1536]{1,0:T(4,128)S(1)} %collective-permute-done.3.got_1) | copy-start | bytes 55300
  59.3 0.6 copy-start.4
  65.2 5.0 %collective-permute-start.5 = (f32[8,128]{1,0:T(8,128)}, f32[8,128]{1,0:T(8,128)S(1)}, u32[]{:S(2)}, u32[]{:S(2)}) collective-permute-start(f32[8,128]{1,0:T(8,128)} %get-tuple-element.16), channel_id=1, source_target_pairs={{0,1},{1,2},{2,3},{3,4},{4,5},{5,6},{6,7},{7,8},{8,9},{9,10},{10,1... | collective-permute-start | bytes 12296 | tf_op jit(solution)/shard_map/ppermute | solution.py:438
  67.1 9.6 %collective-permute-start.6 = (f32[8,128]{1,0:T(8,128)}, f32[8,128]{1,0:T(8,128)S(1)}, u32[]{:S(2)}, u32[]{:S(2)}) collective-permute-start(f32[8,128]{1,0:T(8,128)} %get-tuple-element.17), channel_id=1, source_target_pairs={{1,0},{2,1},{3,2},{4,3},{5,4},{6,5},{7,6},{8,7},{9,8},{10,9},{11,1... | collective-permute-start | bytes 12296 | tf_op jit(solution)/shard_map/ppermute | solution.py:439
  70.2 6.5 %copy-start.6 = (f32[8,128]{1,0:T(8,128)}, f32[8,128]{1,0:T(8,128)S(1)}, u32[]{:S(2)}) copy-start(f32[8,128]{1,0:T(8,128)S(1)} %collective-permute-done.5.couple_top) | copy-start | bytes 12292
  76.8 0.6 copy-start.7
where the time goes:
time: 108 us; the launch traced here: 107 us
  Pallas kernels  51.7 us (48%)
  starting transfers between devices  29.9 us (28%)
  waiting for transfers between devices  11.9 us (11%)
  local copies, waits for them, and re-layouts  8.66 us (8%)
  other arithmetic  3.76 us (3%)
    pallas_call x1, Pallas kernels, per_device(): pl.pallas_call(step_kernel, out_shape=(shape(1, ROWS, ROW), shape(1, ROWS...  29.3 us
    pallas_call x1, Pallas kernels, per_device(): pl.pallas_call(first_kernel, out_shape=(shape(2, PAIR_ROWS, ROW), shape(P...  17.2 us
    all_to_all x1, starting transfers between devices, per_device(): stiffest = jnp.max(lax.all_to_all(local, ('grp', 'patch'), 0, 0)).reshape(1)  9.29 us
    ppermute x1, starting transfers between devices, per_device(): halo_top = lax.ppermute(last_rows, 'patch', down)  7.49 us
    unnamed x22, local copies, waits for them, and re-layouts  6.65 us
    ppermute x1, waiting for transfers between devices, per_device(): couple_bottom = lax.ppermute(edge_top, 'patch', up)  6.53 us
    ppermute x3, starting transfers between devices, per_device(): got.append(lax.ppermute(sends[2 - j], both, pairs))  6.23 us
    ppermute x3, waiting for transfers between devices, per_device(): got.append(lax.ppermute(sends[2 - j], both, pairs))  5.31 us
  transfers between devices with their start and end apart: 8, of which 2 were waited for; matrix products, arithmetic and copies ran while one was open for 7% of the time, Pallas kernels for 21%

commit v1 on v0

v1 whole, which is shorter than its diff:
```python
import jax
import jax.numpy as jnp
from jax import lax
from jax.experimental import pallas as pl
from jax.experimental.pallas import tpu as pltpu
from jax.sharding import PartitionSpec as P

POINTS = 128
REACH = 2
SUBSTEPS = 4
EDGE = 3
COURANT = 0.4
ROWS = 2048
ROW = 384
SLOTS = 1536
HALO = 8
RUN = 129
PAIRS = 65
PLANE = 2080
TOP = 8
PAIR_ROWS = PAIRS * 16
BAND_ROWS = (PAIRS + 2) * 16
CHUNK = 208
CHUNK_PAIRS = CHUNK // 16
F32 = jnp.float32
BF16 = jnp.bfloat16


def dot(a, b):
    return jnp.dot(a, b, preferred_element_type=F32)


def dot_nt(a, b):
    return lax.dot_general(a, b, (((1,), (1,)), ((), ())), preferred_element_type=F32)


def cols(c):
    return slice(c * 128, (c + 1) * 128)


def band_copies(stiff, wide_a, wide_b, wide_c, sem):
    copies = []
    for b in range(5):
        rows = pl.ds(b * ROW, ROW)
        next_rows = pl.ds((b + 1) * ROW, ROW)
        copies.append((stiff.at[b, :, pl.ds(0, 256)], wide_a.at[rows, :]))
        copies.append((stiff.at[b, :, pl.ds(256, 128)], wide_b.at[rows, pl.ds(0, 128)]))
        copies.append((stiff.at[b, :, pl.ds(0, 128)], wide_b.at[next_rows, pl.ds(128, 128)]))
        copies.append((stiff.at[b, :, pl.ds(128, 256)], wide_c.at[rows, :]))
    return [pltpu.make_async_copy(src, dst, sem.at[i]) for i, (src, dst) in enumerate(copies)]


def band_zeros(wide_b):
    wide_b[5 * ROW : 6 * ROW, 0:128] = jnp.zeros((ROW, 128), BF16)
    wide_b[0:ROW, 128:256] = jnp.zeros((ROW, 128), BF16)


def band_products(operand, start, wide_a, wide_b, wide_c):
    parts = [operand[i % 2, pl.ds(start + (i // 2) * 16, CHUNK), :] for i in range(6)]
    part_a = dot(jnp.concatenate(parts[:5], axis=1), wide_a[...])
    part_b = dot(jnp.concatenate(parts, axis=1), wide_b[...])
    part_c = dot(jnp.concatenate(parts[1:], axis=1), wide_c[...])
    even = [part_a[:, 0:128], part_a[:, 128:256], part_b[:, 0:128]]
    odd = [part_b[:, 128:256], part_c[:, 0:128], part_c[:, 128:256]]
    return even, odd


def put_halo(plane, near, far, even, first, count):
    for c in range(count):
        column = slice(first + c * 128, first + c * 128 + 128)
        plane[c, TOP : TOP + HALO, :] = jnp.where(even, far[:, column], near[:, column])
        plane[c, TOP + HALO + ROWS : TOP + 2 * HALO + ROWS, :] = jnp.where(even, near[:, column], far[:, column])
        plane[c, 0:TOP, :] = jnp.zeros((TOP, 128), F32)
        plane[c, PLANE - 8 : PLANE, :] = jnp.zeros((8, 128), F32)


def plane_copies(array, plane, count, sem):
    return [
        pltpu.make_async_copy(
            array.at[0, :, pl.ds(c * 128, 128)], plane.at[c, pl.ds(TOP + HALO, ROWS), :], sem.at[c]
        )
        for c in range(count)
    ]


def spread(k):
    return pl.ds(TOP + k, 16, stride=RUN)


def bundle_kernel(displace, velocity, ext_force, inv_mass, thickness, near_rows, far_rows, sem):
    even = lax.axis_index("patch") % 2 == 0
    copies = []
    last = ROWS - HALO
    near_start = pl.multiple_of(jnp.where(even, last, 0), 8)
    far_start = pl.multiple_of(jnp.where(even, 0, last), 8)
    column = 0
    for array in [displace, velocity, ext_force, inv_mass, thickness]:
        width = array.shape[2]
        for rows, out in [(far_start, far_rows), (near_start, near_rows)]:
            copies.append(
                pltpu.make_async_copy(
                    array.at[0, pl.ds(rows, HALO), :], out.at[:, pl.ds(column, width)], sem.at[len(copies)]
                )
            )
        column += width
    for copy in copies:
        copy.start()
    for copy in copies:
        copy.wait()


def fill_operand(field, operand, step):
    for half in range(2):
        for c in range(3):
            operand[half, pl.ds(step * 16, 16), cols(c)] = field[c, spread(2 * step + half - 2), :].astype(BF16)


def load_kernel(displace, stiff, field, operand, wide_a, wide_b, wide_c, sem_field, sem_band):
    field_in = plane_copies(displace, field, 3, sem_field)
    bands_in = band_copies(stiff, wide_a, wide_b, wide_c, sem_band)
    for copy in field_in + bands_in:
        copy.start()
    for c in range(3):
        field[c, 0 : TOP + HALO, :] = jnp.zeros((TOP + HALO, 128), F32)
        field[c, TOP + HALO + ROWS : PLANE, :] = jnp.zeros((PLANE - TOP - HALO - ROWS, 128), F32)
    band_zeros(wide_b)
    for copy in field_in:
        copy.wait()

    def some(i, carry):
        for j in range(4):
            fill_operand(field, operand, pl.multiple_of(i * 4, 4) + j + 3)
        return carry

    for step in range(3):
        fill_operand(field, operand, step)
    lax.fori_loop(0, (PAIRS - 1) // 4, some, 0)
    for copy in bands_in:
        copy.wait()


def slot_place(entry):
    row = (entry * 21846) >> 16
    return row >> 7, row & 127, entry - 3 * row


def first_kernel(
    field_in, operand_in, wide_a, wide_b, wide_c, near_rows, far_rows, points,
    velocity, ext_force, inv_mass, thickness,
    field, operand, moving, outer, mass, thick, force, compact, stiffest, send_far, send_mid, send_near,
    table, sem_moving, sem_outer, sem_mass, sem_thick,
):
    even = lax.axis_index("patch") % 2 == 0
    near_j = jnp.where(even, 2, 0)
    thick_in = plane_copies(thickness, thick, 1, sem_thick)
    moving_in = plane_copies(velocity, moving, 3, sem_moving)
    mass_in = plane_copies(inv_mass, mass, 1, sem_mass)
    outer_in = plane_copies(ext_force, outer, 3, sem_outer)
    for copy in thick_in + moving_in + mass_in + outer_in:
        copy.start()
    put_halo(field, near_rows, far_rows, even, 0, 3)
    put_halo(moving, near_rows, far_rows, even, 384, 3)
    put_halo(outer, near_rows, far_rows, even, 768, 3)
    put_halo(mass, near_rows, far_rows, even, 1152, 1)
    put_halo(thick, near_rows, far_rows, even, 1280, 1)
    for step in list(range(6)) + list(range(60, 67)):
        fill_operand(field, operand, step)
    lane = lax.broadcasted_iota(jnp.int32, (16, 128), 1)

    def make_compact(start, results):
        for i in range(CHUNK_PAIRS):
            for half in range(2):
                at = spread(2 * (start // 16 + i) + half)
                half_thick = 0.5 * thick[0, at, :]
                parts = [
                    field[c, at, :]
                    + 0.5 * moving[c, at, :]
                    + half_thick * results[half][c][i * 16 : i * 16 + 16, :]
                    for c in range(3)
                ]
                compact[at, :] = jnp.where(
                    lane < 3,
                    parts[0],
                    jnp.where(lane < 6, pltpu.roll(parts[1], 3, 1), pltpu.roll(parts[2], 6, 1)),
                )

    before = None
    for start in range(0, PAIR_ROWS, CHUNK):
        results = band_products(operand, start, wide_a, wide_b, wide_c)
        for half in range(2):
            for c in range(3):
                force[half, start : start + CHUNK, cols(c)] = results[half][c]
        if before is None:
            for copy in thick_in + moving_in:
                copy.wait()
        else:
            make_compact(*before)
        before = (start, results)
    make_compact(*before)
    for group in range(16):
        start = TOP + HALO + group * 128
        turned = compact[start : start + 128, :].T[0:16, :]
        high = turned.astype(BF16)
        table[group * 16 : group * 16 + 16, 0:128] = high
        table[group * 16 : group * 16 + 16, 128:256] = (turned - high.astype(F32)).astype(BF16)
    place = lax.broadcasted_iota(jnp.int32, (128, SLOTS), 0)
    for j, send in [(2 - near_j, send_far), (1, send_mid), (near_j, send_near)]:
        group_of, low, point = slot_place(points[j])
        chosen = jnp.where(place == low, 1.0, 0.0).astype(BF16)
        picked = dot(table[...], jnp.concatenate([chosen, chosen], axis=0))
        total = jnp.zeros((16, SLOTS), F32)
        for group in range(16):
            total = total + jnp.where(group_of == group, picked[group * 16 : group * 16 + 16, :], 0.0)
        for c in range(3):
            send[c] = jnp.where(
                point == 0,
                total[3 * c : 3 * c + 1, :],
                jnp.where(point == 1, total[3 * c + 1 : 3 * c + 2, :], total[3 * c + 2 : 3 * c + 3, :]),
            )
    for copy in mass_in:
        copy.wait()
    product = jnp.zeros((8, 128), F32)
    for i in range(8):
        rows = slice(TOP + HALO + i * 256, TOP + HALO + i * 256 + 256)
        product = jnp.maximum(
            product, jnp.max((mass[0, rows, :] * thick[0, rows, :]).reshape(32, 8, 128), axis=0)
        )
    stiffest[...] = product
    for copy in outer_in:
        copy.wait()


def couple_kernel(got_far, got_mid, got_near, points, weights, compact, stiffest, coupling, parcel, total):
    group_here = lax.axis_index("grp")
    block = lax.axis_index("patch")
    blocks = lax.axis_size("patch")
    place = lax.broadcasted_iota(jnp.int32, (128, SLOTS), 0)
    line = lax.broadcasted_iota(jnp.int32, (16, SLOTS), 0)
    summed = None
    near_j = jnp.where(block % 2 == 0, 2, 0)
    for j, got in [(2 - near_j, got_far), (1, got_mid), (near_j, got_near)]:
        group_of, low, point = slot_place(points[j])
        neighbour = block + (j - 1)
        present = jnp.where((neighbour >= 0) & (neighbour < blocks), 1.0, 0.0)
        weight = weights[j] * present
        spread_out = jnp.zeros((16, SLOTS), F32)
        for c in range(4):
            value = weight * got[c] if c < 3 else weight
            spread_out = jnp.where(line == 3 * c + point, value, spread_out)
        high = spread_out.astype(BF16)
        rest = (spread_out - high.astype(F32)).astype(BF16)
        zero = jnp.zeros((16, SLOTS), BF16)
        right = jnp.concatenate(
            [jnp.where(group_of == group, high, zero) for group in range(16)]
            + [jnp.where(group_of == group, rest, zero) for group in range(16)],
            axis=0,
        )
        chosen = jnp.where(place == low, 1.0, 0.0).astype(BF16)
        part = dot_nt(chosen, right)
        summed = part if summed is None else summed + part
    total[...] = summed[:, 0:256] + summed[:, 256:512]
    lane = lax.broadcasted_iota(jnp.int32, (128, 128), 1)
    edges = []
    for group in range(16):
        half = total[:, (group // 8) * 128 : (group // 8) * 128 + 128]
        shift = (group % 8) * 16
        block_sum = pltpu.roll(half, 128 - shift, 1) if shift else half
        weight_sum = jnp.where(
            lane < 3,
            pltpu.roll(block_sum, 119, 1),
            jnp.where(lane < 6, pltpu.roll(block_sum, 122, 1), pltpu.roll(block_sum, 125, 1)),
        )
        start = TOP + HALO + group * 128
        here = block_sum - compact[start : start + 128, :] * weight_sum
        here = jnp.where(lane < 9, here, 0.0)
        coupling[group * 128 : group * 128 + 128, :] = here
        if group == 0:
            edges.append(here[0:8, :])
        if group == 15:
            edges.append(here[120:128, :])
    lane_row = lax.broadcasted_iota(jnp.int32, (1, 128), 1)
    most = jnp.max(jnp.max(stiffest[...], axis=0, keepdims=True), axis=1, keepdims=True)
    flat = []
    for edge in edges:
        line_up = edge[0:1, :]
        for row in range(1, 8):
            line_up = line_up + pltpu.roll(edge, 16 * row, 1)[row : row + 1, :]
        flat.append(jnp.where(lane_row == 15, most, line_up))
    parcel[...] = jnp.broadcast_to(flat[0][None], (128, 1, 128))
    here_index = group_here * blocks + block
    parcel[jnp.minimum(here_index + 1, 2 * blocks - 1)] = flat[1]


def step_kernel(
    parcel, field, moving, outer, mass, thick, force, coupling, wide_a, wide_b, wide_c,
    new_field, new_moving,
    couple, state, speed, push, drag, operand_a, operand_b, place_out, speed_out, sem_out,
):
    group_here = lax.axis_index("grp")
    block = lax.axis_index("patch")
    blocks = lax.axis_size("patch")
    fine = group_here == 1
    lane_row = lax.broadcasted_iota(jnp.int32, (1, 128), 1)
    sublane = lax.broadcasted_iota(jnp.int32, (8, 128), 0)
    most = jnp.max(parcel[...].reshape(2 * blocks, 128), axis=0, keepdims=True)
    most = jnp.max(jnp.where(lane_row == 15, most, 0.0), axis=1, keepdims=True)
    limit = jnp.broadcast_to(most, (16, 128))
    base_step = COURANT * (1.0 / jnp.sqrt(limit))
    size = jnp.where(fine, base_step, SUBSTEPS * base_step)
    square = size * size
    inverse = 1.0 / size
    here_index = group_here * blocks + block
    for start, there, exists in [
        (TOP, jnp.maximum(here_index - 1, 0), block > 0),
        (TOP + HALO + ROWS, jnp.minimum(here_index + 1, 2 * blocks - 1), block < blocks - 1),
    ]:
        line_up = jnp.broadcast_to(parcel[there], (8, 128))
        edge = line_up
        for row in range(1, 8):
            edge = jnp.where(sublane == row, pltpu.roll(line_up, 128 - 16 * row, 1), edge)
        couple[start : start + 8, :] = jnp.where(exists, edge, 0.0)
    couple[TOP + HALO : TOP + HALO + ROWS, :] = coupling[...]
    couple[0:TOP, :] = jnp.zeros((TOP, 128), F32)
    couple[PLANE - 8 : PLANE, :] = jnp.zeros((8, 128), F32)
    lane = lax.broadcasted_iota(jnp.int32, (16, 128), 1)

    def first_step(turn, carry):
        for i in range(5):
            step = turn * 5 + i
            for half in range(2):
                at = spread(2 * step + half)
                tile = pl.ds(pl.multiple_of(step * 16, 16), 16)
                next_tile = pl.ds(pl.multiple_of(step * 16 + 16, 16), 16)
                scaled = square * mass[0, at, :]
                pull = scaled * thick[0, at, :]
                drag[half, tile, :] = pull
                both = couple[at, :]
                for c in range(3):
                    here = jnp.where(lane < 3, pltpu.roll(both, 128 - 3 * c, 1) if c else both, 0.0)
                    drive = scaled * (outer[c, at, :] + here)
                    push[half, tile, cols(c)] = drive
                    new_speed = size * moving[c, at, :] + (drive - pull * force[half, tile, cols(c)])
                    place = field[c, at, :] + new_speed
                    speed[half, tile, cols(c)] = new_speed
                    state[half, tile, cols(c)] = place
                    operand_a[half, next_tile, cols(c)] = place.astype(BF16)
        return carry

    lax.fori_loop(0, PAIRS // 5, first_step, 0)

    def fill_ends(operand):
        for c in range(3):
            operand[0, 0:16, cols(c)] = pltpu.roll(state[1, 63 * 16 : 64 * 16, cols(c)], 1, 0).astype(BF16)
            operand[1, 0:16, cols(c)] = pltpu.roll(state[0, 64 * 16 : 65 * 16, cols(c)], 1, 0).astype(BF16)
            operand[0, 66 * 16 : 67 * 16, cols(c)] = pltpu.roll(state[1, 0:16, cols(c)], 15, 0).astype(BF16)
            operand[1, 66 * 16 : 67 * 16, cols(c)] = pltpu.roll(state[0, 16:32, cols(c)], 15, 0).astype(BF16)

    def substep(operand, following):
        def update(start, results):
            rows = slice(start, start + CHUNK)
            for half in range(2):
                pull = drag[half, rows, :]
                for c in range(3):
                    new_speed = speed[half, rows, cols(c)] + (push[half, rows, cols(c)] - pull * results[half][c])
                    place = state[half, rows, cols(c)] + new_speed
                    if following is not None:
                        speed[half, rows, cols(c)] = new_speed
                        state[half, rows, cols(c)] = place
                        following[half, start + 16 : start + 16 + CHUNK, cols(c)] = place.astype(BF16)
                    else:
                        for i in range(CHUNK_PAIRS):
                            at = spread(2 * (start // 16 + i) + half)
                            place_out[c, at, :] = place[i * 16 : i * 16 + 16, :]
                            speed_out[c, at, :] = new_speed[i * 16 : i * 16 + 16, :] * inverse

        before = None
        for start in range(0, PAIR_ROWS, CHUNK):
            results = band_products(operand, start, wide_a, wide_b, wide_c)
            if before is not None:
                update(*before)
            before = (start, results)
        update(*before)

    @pl.when(fine)
    def _():
        fill_ends(operand_a)
        substep(operand_a, operand_b)
        fill_ends(operand_b)
        substep(operand_b, operand_a)
        fill_ends(operand_a)
        substep(operand_a, None)

    @pl.when(jnp.logical_not(fine))
    def _():
        def last(turn, carry):
            for i in range(5):
                step = turn * 5 + i
                for half in range(2):
                    at = spread(2 * step + half)
                    tile = pl.ds(pl.multiple_of(step * 16, 16), 16)
                    for c in range(3):
                        place_out[c, at, :] = state[half, tile, cols(c)]
                        speed_out[c, at, :] = speed[half, tile, cols(c)] * inverse
            return carry

        lax.fori_loop(0, PAIRS // 5, last, 0)

    out = []
    for c in range(3):
        inner = pl.ds(TOP + HALO, ROWS)
        out.append(
            pltpu.make_async_copy(place_out.at[c, inner, :], new_field.at[0, :, pl.ds(c * 128, 128)], sem_out.at[c])
        )
        out.append(
            pltpu.make_async_copy(speed_out.at[c, inner, :], new_moving.at[0, :, pl.ds(c * 128, 128)], sem_out.at[3 + c])
        )
    for copy in out:
        copy.start()
    for copy in out:
        copy.wait()


ANY = pl.BlockSpec(memory_space=pl.ANY)
IN_VMEM = pl.BlockSpec(memory_space=pltpu.VMEM)
DMA = pltpu.SemaphoreType.DMA
PLANE_3 = pltpu.VMEM((3, PLANE, 128), F32)
PLANE_1 = pltpu.VMEM((1, PLANE, 128), F32)
FULL = pltpu.VMEM((2, PAIR_ROWS, ROW), F32)
OPERAND = pltpu.VMEM((2, BAND_ROWS, ROW), BF16)
BANDS = [
    pltpu.VMEM((5 * ROW, 256), BF16),
    pltpu.VMEM((6 * ROW, 256), BF16),
    pltpu.VMEM((5 * ROW, 256), BF16),
]


def near(*arrays):
    return [pltpu.with_memory_space_constraint(a, pltpu.VMEM) for a in arrays]


def params(mib):
    return pltpu.CompilerParams(vmem_limit_bytes=mib * 2**20)


def per_device(
    displace, velocity, ext_force, inv_mass, thickness, stiff_bands, pair_points, pair_weights
):
    blocks = lax.axis_size("patch")
    points = pair_points.reshape(3, 1, SLOTS)
    weights = pair_weights.reshape(3, 1, SLOTS)
    near_pairs = [(i, i ^ 1) for i in range(blocks)]
    far_pairs = [(i, i + 1 if i % 2 else i - 1) for i in range(1, blocks - 1)]
    width = 3 * ROW + 2 * POINTS
    near_rows, far_rows = pl.pallas_call(
        bundle_kernel,
        out_shape=(pltpu.VMEM((HALO, width), F32), pltpu.VMEM((HALO, width), F32)),
        in_specs=[ANY] * 5,
        out_specs=[IN_VMEM] * 2,
        scratch_shapes=[DMA((10,))],
        compiler_params=params(2),
        name="bundle",
    )(*[pltpu.with_memory_space_constraint(a, pltpu.HBM) for a in [displace, velocity, ext_force, inv_mass, thickness]])
    far_rows = lax.ppermute(far_rows, "patch", far_pairs)
    near_rows = lax.ppermute(near_rows, "patch", near_pairs)

    field, operand, *bands = pl.pallas_call(
        load_kernel,
        out_shape=(PLANE_3, OPERAND, *BANDS),
        in_specs=[ANY] * 2,
        out_specs=[IN_VMEM] * 5,
        scratch_shapes=[DMA((3,)), DMA((20,))],
        compiler_params=params(2),
        name="load",
    )(displace, stiff_bands)

    slots = pltpu.VMEM((3, 1, SLOTS), F32)
    field, operand, moving, outer, mass, thick, force, compact, stiffest, *sends = pl.pallas_call(
        first_kernel,
        out_shape=(
            PLANE_3, OPERAND, PLANE_3, PLANE_3, PLANE_1, PLANE_1, FULL,
            pltpu.VMEM((PLANE, 128), F32), pltpu.VMEM((8, 128), F32), slots, slots, slots,
        ),
        in_specs=[IN_VMEM] * 8 + [ANY] * 4,
        out_specs=[IN_VMEM] * 12,
        scratch_shapes=[pltpu.VMEM((256, 256), BF16), DMA((3,)), DMA((3,)), DMA((1,)), DMA((1,))],
        input_output_aliases={0: 0, 1: 1},
        compiler_params=params(16),
        name="first_force",
    )(
        *near(field, operand, *bands, near_rows, far_rows, points),
        velocity, ext_force, inv_mass, thickness,
    )

    both = ("grp", "patch")
    mid_pairs = [(i, i) for i in range(blocks)]
    got = [
        lax.ppermute(
            send, both, [(g * blocks + i, (1 - g) * blocks + t) for g in range(2) for i, t in pairs]
        )
        for send, pairs in zip(sends, [far_pairs, mid_pairs, near_pairs])
    ]

    coupling, parcel = pl.pallas_call(
        couple_kernel,
        out_shape=(pltpu.VMEM((ROWS, 128), F32), pltpu.VMEM((2 * blocks, 1, 128), F32)),
        in_specs=[IN_VMEM] * 7,
        out_specs=[IN_VMEM] * 2,
        scratch_shapes=[pltpu.VMEM((128, 256), F32)],
        compiler_params=params(16),
        name="couple",
    )(*near(*got, points, weights, compact, stiffest))
    parcel = lax.all_to_all(parcel, both, 0, 0)

    new_field, new_moving = pl.pallas_call(
        step_kernel,
        out_shape=(
            jax.ShapeDtypeStruct((1, ROWS, ROW), F32),
            jax.ShapeDtypeStruct((1, ROWS, ROW), F32),
        ),
        in_specs=[IN_VMEM] * 11,
        out_specs=[ANY] * 2,
        scratch_shapes=[pltpu.VMEM((PLANE, 128), F32), FULL, FULL, FULL, pltpu.VMEM((2, PAIR_ROWS, 128), F32)]
        + [OPERAND, OPERAND, PLANE_3, PLANE_3, DMA((6,))],
        compiler_params=params(28),
        name="steps",
    )(*near(parcel, field, moving, outer, mass, thick, force, coupling, *bands))
    return new_field, new_moving


def solution(mesh):
    spec3 = P("grp", "patch", None)
    spec4 = P("grp", "patch", None, None)
    return jax.shard_map(
        per_device,
        mesh=mesh,
        in_specs=(spec3, spec3, spec3, spec3, spec3, P(), spec4, spec4),
        out_specs=(spec3, spec3),
        check_vma=False,
    )
```

time: 108 us -> 66.5 us (0.62)
  the two profiles are of different devices: /device:TPU:121 before, /device:TPU:33 now
where the time goes in v1:
time: 66.5 us; the launch traced here: 66.3 us
  Pallas kernels  28.2 us (42%)
  blocking collectives  24.3 us (37%)
  starting transfers between devices  8.37 us (13%)
  waiting for transfers between devices  4.4 us (7%)
  between operations  0.95 us (1%)
    all_to_all x1, blocking collectives, per_device(): parcel = lax.all_to_all(parcel, both, 0, 0)  24.3 us
    pallas_call x1, Pallas kernels, per_device(): pl.pallas_call(step_kernel, out_shape=(jax.ShapeDtypeStruct((1, ROWS, ROW...  16.5 us
    pallas_call x1, Pallas kernels, per_device(): pl.pallas_call(first_kernel, out_shape=(PLANE_3, OPERAND, PLANE_3, PLANE_...  6.67 us
    ppermute x3, starting transfers between devices, per_device(): lax.ppermute(send, both, [(g * blocks + i, (1 - g) * blocks + t) for g in...  4.25 us
    ppermute x1, starting transfers between devices, per_device(): far_rows = lax.ppermute(far_rows, 'patch', far_pairs)  3.37 us
    ppermute x3, waiting for transfers between devices, per_device(): lax.ppermute(send, both, [(g * blocks + i, (1 - g) * blocks + t) for g in...  3.18 us
    pallas_call x1, Pallas kernels, per_device(): pl.pallas_call(couple_kernel, out_shape=(pltpu.VMEM((ROWS, 128), F32), pl...  2.93 us
  transfers between devices with their start and end apart: 5, of which 3 were waited for; matrix products, arithmetic and copies ran while one was open for 0% of the time, Pallas kernels for 2%

profile of v1, /device:TPU:33, one launch (start us, length us, event | category | flops | bytes accessed | tf_op | source)
XLA Modules:
  0.0 66.3 jit_solution(6154689408003002785)
XLA Ops:
  0.7 1.0 %bundle.1 = (f32[8,1408]{1,0:T(8,128)S(1)}, f32[8,1408]{1,0:T(8,128)S(1)}) custom-call(f32[1,2048,384]{2,1,0:T(8,128)} %displace.3, f32[1,2048,384]{2,1,0:T(8,128)} %velocity.3, f32[1,2048,384]{2,1,0:T(8,128)} %ext_force.3, f32[1,2048,128]{2,1,0:T(8,128)} %inv_mass.3, f32[1,2048,128]{2,1,0:T(8,128)} %thickness.3), custom_call_target="tpu_custom_call" | custom-call | tf_op jit(solution)/shard_map/bundle/pallas_call | solution.py:454
  1.7 0.0 copy-start
  1.7 0.0 copy-start.3
  1.7 0.0 copy-start.6
  1.7 0.8 %collective-permute-start = (f32[8,1408]{1,0:T(8,128)S(1)}, f32[8,1408]{1,0:T(8,128)S(1)}, u32[]{:S(2)}, u32[]{:S(2)}) collective-permute-start(f32[8,1408]{1,0:T(8,128)S(1)} %get-tuple-element.27), channel_id=1, source_target_pairs={{0,1},{1,0},{2,3},{3,2},{4,5},{5,4},{6,7},{7,6},{8,9},{9,8},{10,11... | collective-permute-start | bytes 135176 | tf_op jit(solution)/shard_map/ppermute | solution.py:464
  2.5 3.4 %collective-permute-start.1 = (f32[8,1408]{1,0:T(8,128)S(1)}, f32[8,1408]{1,0:T(8,128)S(1)}, u32[]{:S(2)}, u32[]{:S(2)}) collective-permute-start(f32[8,1408]{1,0:T(8,128)S(1)} %get-tuple-element.28), channel_id=1, source_target_pairs={{1,2},{2,1},{3,4},{4,3},{5,6},{6,5},{7,8},{8,7},{9,10},{10,9},{11,... | collective-permute-start | bytes 135176 | tf_op jit(solution)/shard_map/ppermute | solution.py:463
  5.9 0.0 copy-done.2
  5.9 0.0 copy-done.5
  5.9 1.1 %load.1 = (f32[3,2080,128]{2,1,0:T(8,128)S(1)}, bf16[2,1072,384]{2,1,0:T(8,128)(2,1)S(1)}, bf16[1920,256]{1,0:T(8,128)(2,1)S(1)}, bf16[2304,256]{1,0:T(8,128)(2,1)S(1)}, bf16[1920,256]{1,0:T(8,128)(2,1)S(1)}) custom-call(f32[1,2048,384]{2,1,0:T(8,128)S(1)} %copy-done.2, bf16[5,384,384]{2,1,0:T(8,128)(2,1)S(1)} %copy-done.5), custom_call_target="tpu_custom_call" | custom-call | tf_op jit(solution)/shard_map/load/pallas_call | solution.py:466
  7.0 0.0 collective-permute-done.near_rows
  7.0 1.2 %collective-permute-done.1.far_rows = f32[8,1408]{1,0:T(8,128)S(1)} collective-permute-done((f32[8,1408]{1,0:T(8,128)S(1)}, f32[8,1408]{1,0:T(8,128)S(1)}, u32[]{:S(2)}, u32[]{:S(2)}) %collective-permute-start.1) | collective-permute-done | bytes 45088 | tf_op jit(solution)/shard_map/ppermute | solution.py:463
  8.3 0.0 copy-done.3
  8.3 0.0 copy-done.6
  8.3 0.0 copy-start.7
  8.3 6.7 %first_force.1 = (f32[3,2080,128]{2,1,0:T(8,128)S(1)}, bf16[2,1072,384]{2,1,0:T(8,128)(2,1)S(1)}, f32[3,2080,128]{2,1,0:T(8,128)S(1)}, f32[3,2080,128]{2,1,0:T(8...) custom-call(f32[3,2080,128]{2,1,0:T(8,128)S(1)} %get-tuple-element.2, ...), custom_call_target="tpu_custom_call", output_to_operand_aliasing={{0}: (0, {}), {1}: (1, {})} | custom-call | tf_op jit(solution)/shard_map/first_force/pallas_call | solution.py:477
  15.0 2.5 %collective-permute-start.2 = (f32[3,1,1536]{2,1,0:T(1,128)S(1)}, f32[3,1,1536]{2,1,0:T(1,128)S(1)}, u32[]{:S(2)}, u32[]{:S(2)}) collective-permute-start(f32[3,1,1536]{2,1,0:T(1,128)S(1)} %get-tuple-element.29), channel_id=1, source_target_pairs={{1,66},{2,65},{3,68},{4,67},{5,70},{6,69},{7,72},{8,71},{9,74},{10... | collective-permute-start | bytes 55304 | tf_op jit(solution)/shard_map/ppermute | solution.py:497
  17.5 1.7 %collective-permute-start.3 = (f32[3,1,1536]{2,1,0:T(1,128)S(1)}, f32[3,1,1536]{2,1,0:T(1,128)S(1)}, u32[]{:S(2)}, u32[]{:S(2)}) collective-permute-start(f32[3,1,1536]{2,1,0:T(1,128)S(1)} %get-tuple-element.30), channel_id=1, source_target_pairs={{0,64},{1,65},{2,66},{3,67},{4,68},{5,69},{6,70},{7,71},{8,72},{9,... | collective-permute-start | bytes 55304 | tf_op jit(solution)/shard_map/ppermute | solution.py:497
  19.2 0.0 collective-permute-start.4
  19.2 1.7 %collective-permute-done.2.got_far = f32[3,1,1536]{2,1,0:T(1,128)S(1)} collective-permute-done((f32[3,1,1536]{2,1,0:T(1,128)S(1)}, f32[3,1,1536]{2,1,0:T(1,128)S(1)}, u32[]{:S(2)}, u32[]{:S(2)}) %collective-permute-start.2) | collective-permute-done | bytes 18464 | tf_op jit(solution)/shard_map/ppermute | solution.py:497
  21.0 0.0 collective-permute-done.3.got_mid
  21.0 1.5 %collective-permute-done.4.got_near = f32[3,1,1536]{2,1,0:T(1,128)S(1)} collective-permute-done((f32[3,1,1536]{2,1,0:T(1,128)S(1)}, f32[3,1,1536]{2,1,0:T(1,128)S(1)}, u32[]{:S(2)}, u32[]{:S(2)}) %collective-permute-start.4) | collective-permute-done | bytes 18464 | tf_op jit(solution)/shard_map/ppermute | solution.py:497
  22.4 2.9 %couple.1 = (f32[2048,128]{1,0:T(8,128)S(1)}, f32[128,1,128]{2,1,0:T(1,128)S(1)}) custom-call(f32[3,1,1536]{2,1,0:T(1,128)S(1)} %collective-permute-done.2.got_far, f32[3,1,1536]{2,1,0:T(1,128)S(1)} %collective-permute-done.3.got_mid, f32[3,1,1536]{2,1,0:T(1,128)S(1)} %collective-permute-done.4.got_near, s32[3,1,1536]{2,1,0:T(1,128)S(1)} %bitcast.3, ...), custom_call_target="tpu_custom_call" | custom-call | tf_op jit(solution)/shard_map/couple/pallas_call | solution.py:503
  25.3 24.3 %all_to_all.5.parcel = f32[128,1,128]{2,1,0:T(1,128)S(1)} all-to-all(f32[128,1,128]{2,1,0:T(1,128)S(1)} %get-tuple-element.34), channel_id=1, replica_groups=mesh['grp'=2,'patch'=64] {'grp','patch'}, dimensions={0} | all-to-all | bytes 131072 | tf_op jit(solution)/shard_map/all_to_all | solution.py:512
  49.6 16.5 %steps.1 = (f32[1,2048,384]{2,1,0:T(8,128)}, f32[1,2048,384]{2,1,0:T(8,128)}) custom-call(f32[128,1,128]{2,1,0:T(1,128)S(1)} %all_to_all.5.parcel, f32[3,2080,128]{2,1,0:T(8,128)S(1)} %get-tuple-element.35.field, f32[3,2080,128]{2,1,0:T(8,128)S(1)} %get-tuple-element.36.moving, f32[3,2080,128]{2,1,0:T(8,128)S(1)} %get-tuple-element.37.outer, ...), custom_call_target="tpu_custom_call" | custom-call | tf_op jit(solution)/shard_map/steps/pallas_call | solution.py:514
  (8 shorter events, 0.0 us)
Async XLA Ops:
  0.6 5.3 %copy-start.2 = (f32[1,2048,384]{2,1,0:T(8,128)S(1)}, f32[1,2048,384]{2,1,0:T(8,128)}, u32[]{:S(2)}) copy-start(f32[1,2048,384]{2,1,0:T(8,128)} %displace.3) | copy-start | bytes 9437188
  0.6 5.3 %copy-start.5 = (bf16[5,384,384]{2,1,0:T(8,128)(2,1)S(1)}, bf16[5,384,384]{2,1,0:T(8,128)(2,1)}, u32[]{:S(2)}) copy-start(bf16[5,384,384]{2,1,0:T(8,128)(2,1)} %stiff.1) | copy-start | bytes 4423684
  0.7 7.6 %copy-start.1 = (f32[1,2048,384]{2,1,0:T(8,128)S(1)}, f32[1,2048,384]{2,1,0:T(8,128)}, u32[]{:S(2)}) copy-start(f32[1,2048,384]{2,1,0:T(8,128)} %ext_force.3) | copy-start | bytes 9437188
  0.7 7.6 %copy-start.4 = (f32[1,2048,128]{2,1,0:T(8,128)S(1)}, f32[1,2048,128]{2,1,0:T(8,128)}, u32[]{:S(2)}) copy-start(f32[1,2048,128]{2,1,0:T(8,128)} %thickness.3) | copy-start | bytes 3145732
  1.7 6.5 %copy-start = (f32[1,2048,384]{2,1,0:T(8,128)S(1)}, f32[1,2048,384]{2,1,0:T(8,128)}, u32[]{:S(2)}) copy-start(f32[1,2048,384]{2,1,0:T(8,128)} %velocity.3) | copy-start | bytes 9437188
  1.7 6.5 %copy-start.3 = (f32[1,2048,128]{2,1,0:T(8,128)S(1)}, f32[1,2048,128]{2,1,0:T(8,128)}, u32[]{:S(2)}) copy-start(f32[1,2048,128]{2,1,0:T(8,128)} %inv_mass.3) | copy-start | bytes 3145732
  1.7 6.5 %copy-start.6 = (s32[1,1,3,1536]{3,1,2,0:T(1,128)S(1)}, s32[1,1,3,1536]{3,1,2,0:T(1,128)}, u32[]{:S(2)}) copy-start(s32[1,1,3,1536]{3,1,2,0:T(1,128)} %param.14) | copy-start | bytes 55300
  1.7 5.3 %collective-permute-start = (f32[8,1408]{1,0:T(8,128)S(1)}, f32[8,1408]{1,0:T(8,128)S(1)}, u32[]{:S(2)}, u32[]{:S(2)}) collective-permute-start(f32[8,1408]{1,0:T(8,128)S(1)} %get-tuple-element.27), channel_id=1, source_target_pairs={{0,1},{1,0},{2,3},{3,2},{4,5},{5,4},{6,7},{7,6},{8,9},{9,8},{10,11... | collective-permute-start | bytes 135176 | tf_op jit(solution)/shard_map/ppermute | solution.py:464
  2.5 5.7 %collective-permute-start.1 = (f32[8,1408]{1,0:T(8,128)S(1)}, f32[8,1408]{1,0:T(8,128)S(1)}, u32[]{:S(2)}, u32[]{:S(2)}) collective-permute-start(f32[8,1408]{1,0:T(8,128)S(1)} %get-tuple-element.28), channel_id=1, source_target_pairs={{1,2},{2,1},{3,4},{4,3},{5,6},{6,5},{7,8},{8,7},{9,10},{10,9},{11,... | collective-permute-start | bytes 135176 | tf_op jit(solution)/shard_map/ppermute | solution.py:463
  8.3 14.1 %copy-start.7 = (f32[1,1,3,1536]{3,1,2,0:T(1,128)S(1)}, f32[1,1,3,1536]{3,1,2,0:T(1,128)}, u32[]{:S(2)}) copy-start(f32[1,1,3,1536]{3,1,2,0:T(1,128)} %param.15) | copy-start | bytes 55300
  15.0 6.0 %collective-permute-start.2 = (f32[3,1,1536]{2,1,0:T(1,128)S(1)}, f32[3,1,1536]{2,1,0:T(1,128)S(1)}, u32[]{:S(2)}, u32[]{:S(2)}) collective-permute-start(f32[3,1,1536]{2,1,0:T(1,128)S(1)} %get-tuple-element.29), channel_id=1, source_target_pairs={{1,66},{2,65},{3,68},{4,67},{5,70},{6,69},{7,72},{8,71},{9,74},{10... | collective-permute-start | bytes 55304 | tf_op jit(solution)/shard_map/ppermute | solution.py:497
  17.5 3.4 %collective-permute-start.3 = (f32[3,1,1536]{2,1,0:T(1,128)S(1)}, f32[3,1,1536]{2,1,0:T(1,128)S(1)}, u32[]{:S(2)}, u32[]{:S(2)}) collective-permute-start(f32[3,1,1536]{2,1,0:T(1,128)S(1)} %get-tuple-element.30), channel_id=1, source_target_pairs={{0,64},{1,65},{2,66},{3,67},{4,68},{5,69},{6,70},{7,71},{8,72},{9,... | collective-permute-start | bytes 55304 | tf_op jit(solution)/shard_map/ppermute | solution.py:497
  19.2 3.2 %collective-permute-start.4 = (f32[3,1,1536]{2,1,0:T(1,128)S(1)}, f32[3,1,1536]{2,1,0:T(1,128)S(1)}, u32[]{:S(2)}, u32[]{:S(2)}) collective-permute-start(f32[3,1,1536]{2,1,0:T(1,128)S(1)} %get-tuple-element.31), channel_id=1, source_target_pairs={{0,65},{1,64},{2,67},{3,66},{4,69},{5,68},{6,71},{7,70},{8,73},{9,... | collective-permute-start | bytes 55304 | tf_op jit(solution)/shard_map/ppermute | solution.py:497

commit v2 on v1

v2 whole, which is shorter than its diff:
```python
import jax
import jax.numpy as jnp
from jax import lax
from jax.experimental import pallas as pl
from jax.experimental.pallas import tpu as pltpu
from jax.sharding import PartitionSpec as P

POINTS = 128
REACH = 2
SUBSTEPS = 4
EDGE = 3
COURANT = 0.4
ROWS = 2048
ROW = 384
SLOTS = 1536
HALO = 8
RUN = 129
PAIRS = 65
PLANE = 2080
TOP = 8
PAIR_ROWS = PAIRS * 16
BAND_ROWS = (PAIRS + 2) * 16
CHUNK = 208
CHUNK_PAIRS = CHUNK // 16
F32 = jnp.float32
BF16 = jnp.bfloat16


def dot(a, b):
    return jnp.dot(a, b, preferred_element_type=F32)


def dot_nt(a, b):
    return lax.dot_general(a, b, (((1,), (1,)), ((), ())), preferred_element_type=F32)


def cols(c):
    return slice(c * 128, (c + 1) * 128)


def band_copies(stiff, wide_a, wide_b, wide_c, sem):
    copies = []
    for b in range(5):
        rows = pl.ds(b * ROW, ROW)
        next_rows = pl.ds((b + 1) * ROW, ROW)
        copies.append((stiff.at[b, :, pl.ds(0, 256)], wide_a.at[rows, :]))
        copies.append((stiff.at[b, :, pl.ds(256, 128)], wide_b.at[rows, pl.ds(0, 128)]))
        copies.append((stiff.at[b, :, pl.ds(0, 128)], wide_b.at[next_rows, pl.ds(128, 128)]))
        copies.append((stiff.at[b, :, pl.ds(128, 256)], wide_c.at[rows, :]))
    return [pltpu.make_async_copy(src, dst, sem.at[i]) for i, (src, dst) in enumerate(copies)]


def band_zeros(wide_b):
    wide_b[5 * ROW : 6 * ROW, 0:128] = jnp.zeros((ROW, 128), BF16)
    wide_b[0:ROW, 128:256] = jnp.zeros((ROW, 128), BF16)


def pair_products(parts, wide_a, wide_b, wide_c):
    part_a = dot(jnp.concatenate(parts[:5], axis=1), wide_a[...])
    part_b = dot(jnp.concatenate(parts, axis=1), wide_b[...])
    part_c = dot(jnp.concatenate(parts[1:], axis=1), wide_c[...])
    even = [part_a[:, 0:128], part_a[:, 128:256], part_b[:, 0:128]]
    odd = [part_b[:, 128:256], part_c[:, 0:128], part_c[:, 128:256]]
    return even, odd


def band_products(operand, start, count, wide_a, wide_b, wide_c):
    parts = [operand[i % 2, pl.ds(start + (i // 2) * 16, count), :] for i in range(6)]
    return pair_products(parts, wide_a, wide_b, wide_c)


def put_halo(plane, near, far, even, first, count):
    for c in range(count):
        column = slice(first + c * 128, first + c * 128 + 128)
        plane[c, TOP : TOP + HALO, :] = jnp.where(even, far[:, column], near[:, column])
        plane[c, TOP + HALO + ROWS : TOP + 2 * HALO + ROWS, :] = jnp.where(even, near[:, column], far[:, column])
        plane[c, 0:TOP, :] = jnp.zeros((TOP, 128), F32)
        plane[c, PLANE - 8 : PLANE, :] = jnp.zeros((8, 128), F32)


def plane_copies(array, plane, count, sem):
    return [
        pltpu.make_async_copy(
            array.at[0, :, pl.ds(c * 128, 128)], plane.at[c, pl.ds(TOP + HALO, ROWS), :], sem.at[c]
        )
        for c in range(count)
    ]


def spread(k):
    return pl.ds(TOP + k, 16, stride=RUN)


def bundle_kernel(displace, velocity, ext_force, inv_mass, thickness, near_rows, far_rows, sem):
    even = lax.axis_index("patch") % 2 == 0
    copies = []
    last = ROWS - HALO
    near_start = pl.multiple_of(jnp.where(even, last, 0), 8)
    far_start = pl.multiple_of(jnp.where(even, 0, last), 8)
    column = 0
    for array in [displace, velocity, ext_force, inv_mass, thickness]:
        width = array.shape[2]
        for rows, out in [(far_start, far_rows), (near_start, near_rows)]:
            copies.append(
                pltpu.make_async_copy(
                    array.at[0, pl.ds(rows, HALO), :], out.at[:, pl.ds(column, width)], sem.at[len(copies)]
                )
            )
        column += width
    for copy in copies:
        copy.start()
    for copy in copies:
        copy.wait()


def fill_operand(field, operand, step):
    for half in range(2):
        for c in range(3):
            operand[half, pl.ds(step * 16, 16), cols(c)] = field[c, spread(2 * step + half - 2), :].astype(BF16)


def load_kernel(displace, stiff, near_in, field, operand, wide_a, wide_b, wide_c, near_rows, sem_field, sem_band):
    field_in = plane_copies(displace, field, 3, sem_field)
    bands_in = band_copies(stiff, wide_a, wide_b, wide_c, sem_band)
    for copy in field_in + bands_in:
        copy.start()
    for c in range(3):
        field[c, 0 : TOP + HALO, :] = jnp.zeros((TOP + HALO, 128), F32)
        field[c, TOP + HALO + ROWS : PLANE, :] = jnp.zeros((PLANE - TOP - HALO - ROWS, 128), F32)
    band_zeros(wide_b)
    for copy in field_in:
        copy.wait()

    def some(i, carry):
        for j in range(4):
            fill_operand(field, operand, pl.multiple_of(i * 4, 4) + j + 3)
        return carry

    for step in range(3):
        fill_operand(field, operand, step)
    lax.fori_loop(0, (PAIRS - 1) // 4, some, 0)
    for copy in bands_in:
        copy.wait()


def slot_place(entry):
    row = (entry * 21846) >> 16
    return row >> 7, row & 127, entry - 3 * row


def compact_rows(step, field, moving, thick, compact, force):
    lane = lax.broadcasted_iota(jnp.int32, (16, 128), 1)
    for half in range(2):
        at = spread(2 * step + half)
        half_thick = 0.5 * thick[0, at, :]
        parts = [field[c, at, :] + 0.5 * moving[c, at, :] + half_thick * force[half][c] for c in range(3)]
        compact[at, :] = jnp.where(
            lane < 3,
            parts[0],
            jnp.where(lane < 6, pltpu.roll(parts[1], 3, 1), pltpu.roll(parts[2], 6, 1)),
        )


def some_rows(results, i):
    return [[part[i * 16 : i * 16 + 16, :] for part in half] for half in results]


def force_kernel(
    field, operand, wide_a, wide_b, wide_c, velocity, ext_force, inv_mass, thickness,
    moving, outer, mass, thick, force, compact, stiffest,
    sem_moving, sem_outer, sem_mass, sem_thick,
):
    thick_in = plane_copies(thickness, thick, 1, sem_thick)
    moving_in = plane_copies(velocity, moving, 3, sem_moving)
    mass_in = plane_copies(inv_mass, mass, 1, sem_mass)
    outer_in = plane_copies(ext_force, outer, 3, sem_outer)
    for copy in thick_in + moving_in + mass_in + outer_in:
        copy.start()

    def make_compact(start, results):
        for i in range(CHUNK_PAIRS):
            compact_rows(start // 16 + i, field, moving, thick, compact, some_rows(results, i))

    before = None
    for start in range(0, PAIR_ROWS, CHUNK):
        results = band_products(operand, start, CHUNK, wide_a, wide_b, wide_c)
        for half in range(2):
            for c in range(3):
                force[half, start : start + CHUNK, cols(c)] = results[half][c]
        if before is None:
            for copy in thick_in + moving_in:
                copy.wait()
        else:
            make_compact(*before)
        before = (start, results)
    for copy in mass_in:
        copy.wait()
    product = jnp.zeros((8, 128), F32)
    for i in range(8):
        rows = slice(TOP + HALO + i * 256, TOP + HALO + i * 256 + 256)
        product = jnp.maximum(
            product, jnp.max((mass[0, rows, :] * thick[0, rows, :]).reshape(32, 8, 128), axis=0)
        )
    most = jnp.max(jnp.max(product, axis=0, keepdims=True), axis=1, keepdims=True)
    stiffest[...] = jnp.broadcast_to(most, (8, 128))
    make_compact(*before)
    for copy in outer_in:
        copy.wait()


def pick_slots(entry, table, send):
    place = lax.broadcasted_iota(jnp.int32, (128, SLOTS), 0)
    group_of, low, point = slot_place(entry)
    chosen = jnp.where(place == low, 1.0, 0.0).astype(BF16)
    picked = dot(table[...], jnp.concatenate([chosen, chosen], axis=0))
    total = jnp.zeros((16, SLOTS), F32)
    for group in range(16):
        total = total + jnp.where(group_of == group, picked[group * 16 : group * 16 + 16, :], 0.0)
    for c in range(3):
        send[c] = jnp.where(
            point == 0,
            total[3 * c : 3 * c + 1, :],
            jnp.where(point == 1, total[3 * c + 1 : 3 * c + 2, :], total[3 * c + 2 : 3 * c + 3, :]),
        )


def near_offset():
    return jnp.where(lax.axis_index("patch") % 2 == 0, 2, 0)


FAR_ROWS = 5
LOW_PAIRS = 5
HIGH_PAIR = 59


def ends_kernel(
    wide_a, wide_b, wide_c, near_rows, far_rows, points,
    field_in, operand_in, moving_in, outer_in, mass_in, thick_in, force_in, compact_in,
    field, operand, moving, outer, mass, thick, force, compact, table, send_far,
):
    even = lax.axis_index("patch") % 2 == 0
    put_halo(field, near_rows, far_rows, even, 0, 3)
    put_halo(moving, near_rows, far_rows, even, 384, 3)
    put_halo(outer, near_rows, far_rows, even, 768, 3)
    put_halo(mass, near_rows, far_rows, even, 1152, 1)
    put_halo(thick, near_rows, far_rows, even, 1280, 1)
    for step in list(range(6)) + list(range(60, 67)):
        fill_operand(field, operand, step)
    low = LOW_PAIRS * 16
    high = (PAIRS - HIGH_PAIR) * 16
    parts = [
        jnp.concatenate(
            [
                operand[i % 2, (i // 2) * 16 : (i // 2) * 16 + low, :],
                operand[i % 2, (HIGH_PAIR + i // 2) * 16 : (HIGH_PAIR + i // 2) * 16 + high, :],
            ],
            axis=0,
        )
        for i in range(6)
    ]
    results = pair_products(parts, wide_a, wide_b, wide_c)
    for half in range(2):
        for c in range(3):
            force[half, 0:low, cols(c)] = results[half][c][:low]
            force[half, HIGH_PAIR * 16 : PAIR_ROWS, cols(c)] = results[half][c][low:]
    for i, step in enumerate(list(range(LOW_PAIRS)) + list(range(HIGH_PAIR, PAIRS))):
        compact_rows(step, field, moving, thick, compact, some_rows(results, i))
    for group in range(16):
        start = TOP + HALO + group * 128
        turned = compact[start : start + 128, :].T[0:16, :]
        upper = turned.astype(BF16)
        table[group * 16 : group * 16 + 16, 0:128] = upper
        table[group * 16 : group * 16 + 16, 128:256] = (turned - upper.astype(F32)).astype(BF16)
    pick_slots(points[2 - near_offset()], table, send_far)
    for c in range(3, FAR_ROWS):
        send_far[c] = jnp.zeros((1, SLOTS), F32)


def pick_kernel(table, points, stiffest, send_mid, send_near):
    send_mid[3] = jnp.concatenate([stiffest[0:1, :]] * (SLOTS // 128), axis=1)
    pick_slots(points[1], table, send_mid)
    pick_slots(points[near_offset()], table, send_near)


def sum_slots(j, got, points, weights):
    place = lax.broadcasted_iota(jnp.int32, (128, SLOTS), 0)
    line = lax.broadcasted_iota(jnp.int32, (16, SLOTS), 0)
    group_of, low, point = slot_place(points[j])
    neighbour = lax.axis_index("patch") + (j - 1)
    present = jnp.where((neighbour >= 0) & (neighbour < lax.axis_size("patch")), 1.0, 0.0)
    weight = weights[j] * present
    spread_out = jnp.zeros((16, SLOTS), F32)
    for c in range(4):
        value = weight * got[c] if c < 3 else weight
        spread_out = jnp.where(line == 3 * c + point, value, spread_out)
    high = spread_out.astype(BF16)
    rest = (spread_out - high.astype(F32)).astype(BF16)
    zero = jnp.zeros((16, SLOTS), BF16)
    right = jnp.concatenate(
        [jnp.where(group_of == group, high, zero) for group in range(16)]
        + [jnp.where(group_of == group, rest, zero) for group in range(16)],
        axis=0,
    )
    chosen = jnp.where(place == low, 1.0, 0.0).astype(BF16)
    part = dot_nt(chosen, right)
    return part[:, 0:256] + part[:, 256:512]


def half_couple_kernel(got_mid, got_near, points, weights, stiffest, partial, most):
    partial[...] = sum_slots(1, got_mid, points, weights) + sum_slots(near_offset(), got_near, points, weights)
    most[...] = jnp.maximum(stiffest[...], jnp.broadcast_to(got_mid[3][:, 0:128], (8, 128)))


def couple_kernel(got_far, points, weights, partial, most, compact, coupling, parcel, total):
    block = lax.axis_index("patch")
    blocks = lax.axis_size("patch")
    total[...] = partial[...] + sum_slots(2 - near_offset(), got_far, points, weights)
    lane = lax.broadcasted_iota(jnp.int32, (128, 128), 1)
    edges = []
    for group in range(16):
        half = total[:, (group // 8) * 128 : (group // 8) * 128 + 128]
        shift = (group % 8) * 16
        block_sum = pltpu.roll(half, 128 - shift, 1) if shift else half
        weight_sum = jnp.where(
            lane < 3,
            pltpu.roll(block_sum, 119, 1),
            jnp.where(lane < 6, pltpu.roll(block_sum, 122, 1), pltpu.roll(block_sum, 125, 1)),
        )
        start = TOP + HALO + group * 128
        here = block_sum - compact[start : start + 128, :] * weight_sum
        here = jnp.where(lane < 9, here, 0.0)
        coupling[start : start + 128, :] = here
        if group == 0:
            edges.append(here[0:8, :])
        if group == 15:
            edges.append(here[120:128, :])
    lane_row = lax.broadcasted_iota(jnp.int32, (1, 128), 1)
    flat = []
    for edge in edges:
        line_up = edge[0:1, :]
        for row in range(1, 8):
            line_up = line_up + pltpu.roll(edge, 16 * row, 1)[row : row + 1, :]
        flat.append(jnp.where(lane_row == 15, most[0:1, :], line_up))
    parcel[...] = jnp.broadcast_to(flat[0][None], (blocks, 1, 128))
    parcel[jnp.minimum(block + 1, blocks - 1)] = flat[1]


def step_kernel(
    parcel, field, moving, outer, mass, thick, force, coupling_in, wide_a, wide_b, wide_c,
    new_field, new_moving, couple,
    state, speed, push, drag, operand_a, operand_b, place_out, speed_out, sem_out,
):
    block = lax.axis_index("patch")
    blocks = lax.axis_size("patch")
    fine = lax.axis_index("grp") == 1
    lane_row = lax.broadcasted_iota(jnp.int32, (1, 128), 1)
    sublane = lax.broadcasted_iota(jnp.int32, (8, 128), 0)
    most = jnp.max(parcel[...].reshape(blocks, 128), axis=0, keepdims=True)
    most = jnp.max(jnp.where(lane_row == 15, most, 0.0), axis=1, keepdims=True)
    limit = jnp.broadcast_to(most, (16, 128))
    base_step = COURANT * (1.0 / jnp.sqrt(limit))
    size = jnp.where(fine, base_step, SUBSTEPS * base_step)
    square = size * size
    inverse = 1.0 / size
    for start, there, exists in [
        (TOP, jnp.maximum(block - 1, 0), block > 0),
        (TOP + HALO + ROWS, jnp.minimum(block + 1, blocks - 1), block < blocks - 1),
    ]:
        line_up = jnp.broadcast_to(parcel[there], (8, 128))
        edge = line_up
        for row in range(1, 8):
            edge = jnp.where(sublane == row, pltpu.roll(line_up, 128 - 16 * row, 1), edge)
        edge = jnp.where(lax.broadcasted_iota(jnp.int32, (8, 128), 1) < 9, edge, 0.0)
        couple[start : start + 8, :] = jnp.where(exists, edge, 0.0)
    couple[0:TOP, :] = jnp.zeros((TOP, 128), F32)
    couple[PLANE - 8 : PLANE, :] = jnp.zeros((8, 128), F32)
    lane = lax.broadcasted_iota(jnp.int32, (16, 128), 1)

    def first_update(step, keep):
        for half in range(2):
            at = spread(2 * step + half)
            tile = pl.ds(step * 16, 16) if isinstance(step, int) else pl.ds(pl.multiple_of(step * 16, 16), 16)
            scaled = square * mass[0, at, :]
            pull = scaled * thick[0, at, :]
            both = couple[at, :]
            if keep:
                drag[half, tile, :] = pull
            for c in range(3):
                here = jnp.where(lane < 3, pltpu.roll(both, 128 - 3 * c, 1) if c else both, 0.0)
                drive = scaled * (outer[c, at, :] + here)
                new_speed = size * moving[c, at, :] + (drive - pull * force[half, tile, cols(c)])
                place = field[c, at, :] + new_speed
                if keep:
                    push[half, tile, cols(c)] = drive
                    speed[half, tile, cols(c)] = new_speed
                    state[half, tile, cols(c)] = place
                    operand_a[half, step * 16 + 16 : step * 16 + 32, cols(c)] = place.astype(BF16)
                else:
                    place_out[c, at, :] = place
                    speed_out[c, at, :] = new_speed * inverse

    @pl.when(jnp.logical_not(fine))
    def _():
        def some(turn, carry):
            for i in range(5):
                first_update(turn * 5 + i, False)
            return carry

        lax.fori_loop(0, PAIRS // 5, some, 0)

    def low_ends(operand):
        for c in range(3):
            operand[0, 0:16, cols(c)] = pltpu.roll(state[1, 63 * 16 : 64 * 16, cols(c)], 1, 0).astype(BF16)
            operand[1, 0:16, cols(c)] = pltpu.roll(state[0, 64 * 16 : 65 * 16, cols(c)], 1, 0).astype(BF16)

    def high_ends(operand):
        for c in range(3):
            operand[0, 66 * 16 : 67 * 16, cols(c)] = pltpu.roll(state[1, 0:16, cols(c)], 15, 0).astype(BF16)
            operand[1, 66 * 16 : 67 * 16, cols(c)] = pltpu.roll(state[0, 16:32, cols(c)], 15, 0).astype(BF16)

    def update(chunk, results, following):
        start = chunk * CHUNK
        rows = slice(start, start + CHUNK)
        for half in range(2):
            pull = drag[half, rows, :]
            for c in range(3):
                new_speed = speed[half, rows, cols(c)] + (push[half, rows, cols(c)] - pull * results[half][c])
                place = state[half, rows, cols(c)] + new_speed
                if following is not None:
                    speed[half, rows, cols(c)] = new_speed
                    state[half, rows, cols(c)] = place
                    following[half, start + 16 : start + 16 + CHUNK, cols(c)] = place.astype(BF16)
                else:
                    for i in range(CHUNK_PAIRS):
                        at = spread(2 * (start // 16 + i) + half)
                        place_out[c, at, :] = place[i * 16 : i * 16 + 16, :]
                        speed_out[c, at, :] = new_speed[i * 16 : i * 16 + 16, :] * inverse
        if following is not None and chunk == 0:
            high_ends(following)
        if following is not None and chunk == PAIR_ROWS // CHUNK - 1:
            low_ends(following)

    @pl.when(fine)
    def _():
        for step in [63, 64] + list(range(CHUNK_PAIRS + 1)):
            first_update(step, True)
        low_ends(operand_a)
        high_ends(operand_a)
        before = None
        for operand, following, order in [
            (operand_a, operand_b, [0, 1, 2, 3, 4]),
            (operand_b, operand_a, [1, 2, 3, 4, 0]),
            (operand_a, None, [2, 3, 4, 0, 1]),
        ]:
            for chunk in order:
                results = band_products(operand, chunk * CHUNK, CHUNK, wide_a, wide_b, wide_c)
                if operand is operand_a and following is operand_b:
                    first = (chunk + 1) * CHUNK_PAIRS + 1
                    for step in range(first, min(first + CHUNK_PAIRS, 63)):
                        first_update(step, True)
                if before is not None:
                    update(*before)
                before = (chunk, results, following)
        update(*before)

    out = []
    for c in range(3):
        inner = pl.ds(TOP + HALO, ROWS)
        out.append(
            pltpu.make_async_copy(place_out.at[c, inner, :], new_field.at[0, :, pl.ds(c * 128, 128)], sem_out.at[c])
        )
        out.append(
            pltpu.make_async_copy(speed_out.at[c, inner, :], new_moving.at[0, :, pl.ds(c * 128, 128)], sem_out.at[3 + c])
        )
    for copy in out:
        copy.start()
    for copy in out:
        copy.wait()


ANY = pl.BlockSpec(memory_space=pl.ANY)
IN_VMEM = pl.BlockSpec(memory_space=pltpu.VMEM)
DMA = pltpu.SemaphoreType.DMA
PLANE_3 = pltpu.VMEM((3, PLANE, 128), F32)
PLANE_1 = pltpu.VMEM((1, PLANE, 128), F32)
FULL = pltpu.VMEM((2, PAIR_ROWS, ROW), F32)
OPERAND = pltpu.VMEM((2, BAND_ROWS, ROW), BF16)
BANDS = [
    pltpu.VMEM((5 * ROW, 256), BF16),
    pltpu.VMEM((6 * ROW, 256), BF16),
    pltpu.VMEM((5 * ROW, 256), BF16),
]


def near(*arrays):
    return [pltpu.with_memory_space_constraint(a, pltpu.VMEM) for a in arrays]


def params(mib):
    return pltpu.CompilerParams(vmem_limit_bytes=mib * 2**20)


def per_device(
    displace, velocity, ext_force, inv_mass, thickness, stiff_bands, pair_points, pair_weights
):
    blocks = lax.axis_size("patch")
    points = pair_points.reshape(3, 1, SLOTS)
    weights = pair_weights.reshape(3, 1, SLOTS)
    near_pairs = [(i, i ^ 1) for i in range(blocks)]
    far_pairs = [(i, i + 1 if i % 2 else i - 1) for i in range(1, blocks - 1)]
    width = 3 * ROW + 2 * POINTS
    near_rows, far_rows = pl.pallas_call(
        bundle_kernel,
        out_shape=(pltpu.VMEM((HALO, width), F32), pltpu.VMEM((HALO, width), F32)),
        in_specs=[ANY] * 5,
        out_specs=[IN_VMEM] * 2,
        scratch_shapes=[DMA((10,))],
        compiler_params=params(2),
        name="bundle",
    )(*[pltpu.with_memory_space_constraint(a, pltpu.HBM) for a in [displace, velocity, ext_force, inv_mass, thickness]])
    far_rows = lax.ppermute(far_rows, "patch", far_pairs)

    field, operand, *bands, near_rows = pl.pallas_call(
        load_kernel,
        out_shape=(PLANE_3, OPERAND, *BANDS, pltpu.VMEM((HALO, width), F32)),
        in_specs=[ANY] * 2 + [IN_VMEM],
        out_specs=[IN_VMEM] * 6,
        input_output_aliases={2: 5},
        scratch_shapes=[DMA((3,)), DMA((20,))],
        compiler_params=params(2),
        name="load",
    )(displace, stiff_bands, *near(near_rows))
    near_rows = lax.ppermute(near_rows, "patch", near_pairs)

    plane = pltpu.VMEM((PLANE, 128), F32)
    tile = pltpu.VMEM((8, 128), F32)
    moving, outer, mass, thick, force, compact, stiffest = pl.pallas_call(
        force_kernel,
        out_shape=(PLANE_3, PLANE_3, PLANE_1, PLANE_1, FULL, plane, tile),
        in_specs=[IN_VMEM] * 5 + [ANY] * 4,
        out_specs=[IN_VMEM] * 7,
        scratch_shapes=[DMA((3,)), DMA((3,)), DMA((1,)), DMA((1,))],
        compiler_params=params(12),
        name="force",
    )(*near(field, operand, *bands), velocity, ext_force, inv_mass, thickness)

    slots = pltpu.VMEM((3, 1, SLOTS), F32)
    table = pltpu.VMEM((256, 256), BF16)
    field, operand, moving, outer, mass, thick, force, compact, table, send_far = pl.pallas_call(
        ends_kernel,
        out_shape=(PLANE_3, OPERAND, PLANE_3, PLANE_3, PLANE_1, PLANE_1, FULL, plane, table, pltpu.VMEM((FAR_ROWS, 1, SLOTS), F32)),
        in_specs=[IN_VMEM] * 14,
        out_specs=[IN_VMEM] * 10,
        input_output_aliases={i + 6: i for i in range(8)},
        compiler_params=params(12),
        name="ends",
    )(*near(*bands, near_rows, far_rows, points, field, operand, moving, outer, mass, thick, force, compact))

    both = ("grp", "patch")
    mid_pairs = [(i, i) for i in range(blocks)]

    def across(send, pairs):
        return lax.ppermute(
            send, both, [(g * blocks + i, (1 - g) * blocks + t) for g in range(2) for i, t in pairs]
        )

    got_far = across(send_far, far_pairs)
    send_mid, send_near = pl.pallas_call(
        pick_kernel,
        out_shape=(pltpu.VMEM((4, 1, SLOTS), F32), slots),
        in_specs=[IN_VMEM] * 3,
        out_specs=[IN_VMEM] * 2,
        compiler_params=params(12),
        cost_estimate=pl.CostEstimate(flops=1, transcendentals=0, bytes_accessed=1),
        name="pick",
    )(*near(table, points, stiffest))
    got_mid = across(send_mid, mid_pairs)
    got_near = across(send_near, near_pairs)
    partial, most = pl.pallas_call(
        half_couple_kernel,
        out_shape=(pltpu.VMEM((128, 256), F32), tile),
        in_specs=[IN_VMEM] * 5,
        out_specs=[IN_VMEM] * 2,
        compiler_params=params(12),
        cost_estimate=pl.CostEstimate(flops=1, transcendentals=0, bytes_accessed=1),
        name="half_couple",
    )(*near(got_mid, got_near, points, weights, stiffest))
    coupling, parcel = pl.pallas_call(
        couple_kernel,
        out_shape=(plane, pltpu.VMEM((blocks, 1, 128), F32)),
        in_specs=[IN_VMEM] * 6,
        out_specs=[IN_VMEM] * 2,
        scratch_shapes=[pltpu.VMEM((128, 256), F32)],
        compiler_params=params(12),
        name="couple",
    )(*near(got_far, points, weights, partial, most, compact))
    parcel = lax.all_to_all(parcel, "patch", 0, 0)

    new_field, new_moving, unused = pl.pallas_call(
        step_kernel,
        out_shape=(
            jax.ShapeDtypeStruct((1, ROWS, ROW), F32),
            jax.ShapeDtypeStruct((1, ROWS, ROW), F32),
            pltpu.VMEM((PLANE, 128), F32),
        ),
        in_specs=[IN_VMEM] * 11,
        out_specs=[ANY] * 2 + [IN_VMEM],
        input_output_aliases={7: 2},
        scratch_shapes=[FULL, FULL, FULL, pltpu.VMEM((2, PAIR_ROWS, 128), F32)]
        + [OPERAND, OPERAND, PLANE_3, PLANE_3, DMA((6,))],
        compiler_params=params(28),
        name="steps",
    )(*near(parcel, field, moving, outer, mass, thick, force, coupling, *bands))
    return new_field, new_moving


def solution(mesh):
    spec3 = P("grp", "patch", None)
    spec4 = P("grp", "patch", None, None)
    return jax.shard_map(
        per_device,
        mesh=mesh,
        in_specs=(spec3, spec3, spec3, spec3, spec3, P(), spec4, spec4),
        out_specs=(spec3, spec3),
        check_vma=False,
    )
```

time: 66.5 us -> 62.4 us (0.938)
  blocking collectives: 24.3 us -> 20.3 us
  waiting for transfers between devices: 4.4 us -> 3.19 us
    all_to_all x1, blocking collectives: 24.3 us -> 20.3 us  [per_device(): parcel = lax.all_to_all(parcel, 'patch', 0, 0)]
    pallas_call x3 -> x6, Pallas kernels: 10.7 us -> 12.2 us  [the longest x1 5.08 us: per_device(): pl.pallas_call(force_kernel, out_shape=(PLANE_3, PLANE_3, PLANE_1, PLANE_...]
    ppermute x1, waiting for transfers between devices: 1.22 us -> 0.01 us  [per_device(): far_rows = lax.ppermute(far_rows, 'patch', far_pairs)]
    pallas_call x1, Pallas kernels: 16.5 us -> 15.5 us  [per_device(): pl.pallas_call(step_kernel, out_shape=(jax.ShapeDtypeStruct((1, ROWS, ROW...]
    ppermute x1, starting transfers between devices: 0.75 us -> 0.09 us  [per_device(): near_rows = lax.ppermute(near_rows, 'patch', near_pairs)]
  transfers between devices with their start and end apart: 5 -> 5, of which waited for: 3 -> 1; matrix products, arithmetic and copies ran while one was open for 0% -> 0% of each run, Pallas kernels for 2% -> 13%
where the time goes in v2:
time: 62.4 us; the launch traced here: 62.2 us
  Pallas kernels  28.7 us (46%)
  blocking collectives  20.3 us (33%)
  starting transfers between devices  8.93 us (14%)
  waiting for transfers between devices  3.19 us (5%)
  between operations  1.01 us (2%)
    all_to_all x1, blocking collectives, per_device(): parcel = lax.all_to_all(parcel, 'patch', 0, 0)  20.3 us
    pallas_call x1, Pallas kernels, per_device(): pl.pallas_call(step_kernel, out_shape=(jax.ShapeDtypeStruct((1, ROWS, ROW...  15.5 us
    pallas_call x1, Pallas kernels, per_device(): pl.pallas_call(force_kernel, out_shape=(PLANE_3, PLANE_3, PLANE_1, PLANE_...  5.08 us
    ppermute x3, starting transfers between devices, across(): lax.ppermute(send, both, [(g * blocks + i, (1 - g) * blocks + t) for g in...  4.82 us
    ppermute x1, starting transfers between devices, per_device(): far_rows = lax.ppermute(far_rows, 'patch', far_pairs)  4.03 us
    ppermute x3, waiting for transfers between devices, across(): lax.ppermute(send, both, [(g * blocks + i, (1 - g) * blocks + t) for g in...  3.19 us
    pallas_call x1, Pallas kernels, per_device(): pl.pallas_call(couple_kernel, out_shape=(plane, pltpu.VMEM((blocks, 1, 12...  2.13 us
    pallas_call x1, Pallas kernels, per_device(): pl.pallas_call(ends_kernel, out_shape=(PLANE_3, OPERAND, PLANE_3, PLANE_3...  1.76 us
  transfers between devices with their start and end apart: 5, of which 1 were waited for; matrix products, arithmetic and copies ran while one was open for 0% of the time, Pallas kernels for 13%

profile of v2, /device:TPU:33, one launch (start us, length us, event | category | flops | bytes accessed | tf_op | source)
XLA Modules:
  0.0 62.2 jit_solution(10406195326928078584)
XLA Ops:
  0.7 1.0 %bundle.1 = (f32[8,1408]{1,0:T(8,128)S(1)}, f32[8,1408]{1,0:T(8,128)S(1)}) custom-call(f32[1,2048,384]{2,1,0:T(8,128)} %displace.3, f32[1,2048,384]{2,1,0:T(8,128)} %velocity.3, f32[1,2048,384]{2,1,0:T(8,128)} %ext_force.3, f32[1,2048,128]{2,1,0:T(8,128)} %inv_mass.3, f32[1,2048,128]{2,1,0:T(8,128)} %thickness.3), custom_call_target="tpu_custom_call" | custom-call | tf_op jit(solution)/shard_map/bundle/pallas_call | solution.py:512
  1.7 0.0 copy-start
  1.7 0.0 copy-start.3
  1.7 4.0 %collective-permute-start.1 = (f32[8,1408]{1,0:T(8,128)S(1)}, f32[8,1408]{1,0:T(8,128)S(1)}, u32[]{:S(2)}, u32[]{:S(2)}) collective-permute-start(f32[8,1408]{1,0:T(8,128)S(1)} %get-tuple-element.39), channel_id=1, source_target_pairs={{1,2},{2,1},{3,4},{4,3},{5,6},{6,5},{7,8},{8,7},{9,10},{10,9},{11,... | collective-permute-start | bytes 135176 | tf_op jit(solution)/shard_map/ppermute | solution.py:521
  5.8 1.1 %load.1 = (f32[3,2080,128]{2,1,0:T(8,128)S(1)}, bf16[2,1072,384]{2,1,0:T(8,128)(2,1)S(1)}, bf16[1920,256]{1,0:T(8,128)(2,1)S(1)}, bf16[2304,256]{1,0:T(8,128)(2,...) custom-call(f32[1,2048,384]{2,1,0:T(8,128)S(1)} %copy-done.2, ...), custom_call_target="tpu_custom_call", output_to_operand_aliasing={{5}: (2, {})} | custom-call | tf_op jit(solution)/shard_map/load/pallas_call | solution.py:523
  6.9 0.1 collective-permute-start
  7.0 0.0 copy-done.1
  7.1 0.0 copy-start.6
  7.1 5.1 %force.1 = (f32[3,2080,128]{2,1,0:T(8,128)S(1)}, f32[3,2080,128]{2,1,0:T(8,128)S(1)}, f32[1,2080,128]{2,1,0:T(8,128)S(1)}, f32[1,2080,128]{2,1,0:T(8,128)S(1)}, ...) custom-call(f32[3,2080,128]{2,1,0:T(8,128)S(1)} %get-tuple-element.40.field.field_in, ...), custom_call_target="tpu_custom_call" | custom-call | tf_op jit(solution)/shard_map/force/pallas_call | solution.py:537
  12.2 0.0 collective-permute-done.1.far_rows
  12.2 0.0 collective-permute-done.near_rows
  12.2 0.0 copy-start.7
  12.2 1.8 %ends.1 = (f32[3,2080,128]{2,1,0:T(8,128)S(1)}, bf16[2,1072,384]{2,1,0:T(8,128)(2,1)S(1)}, f32[3,2080,128]{2,1,0:T(8,128)S(1)}, f32[3,2080,128]{2,1,0:T(8,128)S(...) custom-call(bf16[1920,256]{1,0:T(8,128)(2,1)S(1)} %get-tuple-element, ...), custom_call_target="tpu_custom_call", output_to_operand_aliasing={{0}: (6, {}), {1}: (7, {}), {2}: (8, {}), {3}: (9, {}), {4}... | custom-call | tf_op jit(solution)/shard_map/ends/pallas_call | solution.py:549
  14.0 3.1 %collective-permute-start.2 = (f32[5,1,1536]{2,1,0:T(1,128)S(1)}, f32[5,1,1536]{2,1,0:T(1,128)S(1)}, u32[]{:S(2)}, u32[]{:S(2)}) collective-permute-start(f32[5,1,1536]{2,1,0:T(1,128)S(1)} %get-tuple-element.48), channel_id=1, source_target_pairs={{1,66},{2,65},{3,68},{4,67},{5,70},{6,69},{7,72},{8,71},{9,74},{10... | collective-permute-start | bytes 92168 | tf_op jit(solution)/shard_map/ppermute | solution.py:563
  17.1 0.8 %pick.1 = (f32[4,1,1536]{2,1,0:T(1,128)S(1)}, f32[3,1,1536]{2,1,0:T(1,128)S(1)}) custom-call(bf16[256,256]{1,0:T(8,128)(2,1)S(1)} %get-tuple-element.49.table, s32[3,1,1536]{2,1,0:T(1,128)S(1)} %bitcast.3, f32[8,128]{1,0:T(8,128)S(1)} %get-tuple-element.50.stiffest), custom_call_target="tpu_custom_call" | custom-call | flops 1 | bytes 1 | tf_op jit(solution)/shard_map/pick/pallas_call | solution.py:568
  17.9 1.7 %collective-permute-start.3 = (f32[4,1,1536]{2,1,0:T(1,128)S(1)}, f32[4,1,1536]{2,1,0:T(1,128)S(1)}, u32[]{:S(2)}, u32[]{:S(2)}) collective-permute-start(f32[4,1,1536]{2,1,0:T(1,128)S(1)} %get-tuple-element.51), channel_id=1, source_target_pairs={{0,64},{1,65},{2,66},{3,67},{4,68},{5,69},{6,70},{7,71},{8,72},{9,... | collective-permute-start | bytes 73736 | tf_op jit(solution)/shard_map/ppermute | solution.py:563
  19.6 0.0 collective-permute-start.4
  19.6 3.2 %collective-permute-done.4.got_near = f32[3,1,1536]{2,1,0:T(1,128)S(1)} collective-permute-done((f32[3,1,1536]{2,1,0:T(1,128)S(1)}, f32[3,1,1536]{2,1,0:T(1,128)S(1)}, u32[]{:S(2)}, u32[]{:S(2)}) %collective-permute-start.4) | collective-permute-done | bytes 18464 | tf_op jit(solution)/shard_map/ppermute | solution.py:563
  22.8 0.0 collective-permute-done.3.got_mid
  22.8 1.3 %half_couple.1 = (f32[128,256]{1,0:T(8,128)S(1)}, f32[8,128]{1,0:T(8,128)S(1)}) custom-call(f32[4,1,1536]{2,1,0:T(1,128)S(1)} %collective-permute-done.3.got_mid, f32[3,1,1536]{2,1,0:T(1,128)S(1)} %collective-permute-done.4.got_near, s32[3,1,1536]{2,1,0:T(1,128)S(1)} %bitcast.4, f32[3,1,1536]{2,1,0:T(1,128)S(1)} %bitcast.6, ...), custom_call_target="tpu_custom_call" | custom-call | flops 1 | bytes 1 | tf_op jit(solution)/shard_map/half_couple/pallas_call | solution.py:579
  24.1 0.0 collective-permute-done.2.got_far
  24.1 2.1 %couple.1 = (f32[2080,128]{1,0:T(8,128)S(1)}, f32[64,1,128]{2,1,0:T(1,128)S(1)}) custom-call(f32[5,1,1536]{2,1,0:T(1,128)S(1)} %collective-permute-done.2.got_far, s32[3,1,1536]{2,1,0:T(1,128)S(1)} %bitcast.5, f32[3,1,1536]{2,1,0:T(1,128)S(1)} %bitcast.7, f32[128,256]{1,0:T(8,128)S(1)} %get-tuple-element.53.partial, f32[8,128]{1,0:T(8,128)S(1)} %get-tuple-element.54.most, ...), custom_call_target="tpu_custom_call" | custom-call | tf_op jit(solution)/shard_map/couple/pallas_call | solution.py:588
  26.2 20.3 %all_to_all.5.parcel = f32[64,1,128]{2,1,0:T(1,128)S(1)} all-to-all(f32[64,1,128]{2,1,0:T(1,128)S(1)} %get-tuple-element.56), channel_id=1, replica_groups=mesh['grp'=2,'patch'=64] {'patch'}, dimensions={0} | all-to-all | bytes 65536 | tf_op jit(solution)/shard_map/all_to_all | solution.py:597
  46.5 15.5 %steps.1 = (f32[1,2048,384]{2,1,0:T(8,128)}, f32[1,2048,384]{2,1,0:T(8,128)}, f32[2080,128]{1,0:T(8,128)S(1)}) custom-call(f32[64,1,128]{2,1,0:T(1,128)S(1)} %all_to_all.5.parcel, f32[3,2080,128]{2,1,0:T(8,128)S(1)} %get-tuple-element.57.field, f32[3,2080,128]{2,1,0:T(8,128)S(1)} %get-tuple-element.58.moving, ...), custom_call_target="tpu_custom_call", output_to_operand_aliasing={{2}: (7, {})} | custom-call | tf_op jit(solution)/shard_map/steps/pallas_call | solution.py:599
  (11 shorter events, 0.0 us)
Async XLA Ops:
  0.6 5.1 %copy-start.2 = (f32[1,2048,384]{2,1,0:T(8,128)S(1)}, f32[1,2048,384]{2,1,0:T(8,128)}, u32[]{:S(2)}) copy-start(f32[1,2048,384]{2,1,0:T(8,128)} %displace.3) | copy-start | bytes 9437188
  0.6 5.1 %copy-start.5 = (bf16[5,384,384]{2,1,0:T(8,128)(2,1)S(1)}, bf16[5,384,384]{2,1,0:T(8,128)(2,1)}, u32[]{:S(2)}) copy-start(bf16[5,384,384]{2,1,0:T(8,128)(2,1)} %stiff.1) | copy-start | bytes 4423684
  0.7 6.4 %copy-start.1 = (f32[1,2048,384]{2,1,0:T(8,128)S(1)}, f32[1,2048,384]{2,1,0:T(8,128)}, u32[]{:S(2)}) copy-start(f32[1,2048,384]{2,1,0:T(8,128)} %ext_force.3) | copy-start | bytes 9437188
  0.7 6.4 %copy-start.4 = (f32[1,2048,128]{2,1,0:T(8,128)S(1)}, f32[1,2048,128]{2,1,0:T(8,128)}, u32[]{:S(2)}) copy-start(f32[1,2048,128]{2,1,0:T(8,128)} %thickness.3) | copy-start | bytes 3145732
  1.7 5.3 %copy-start = (f32[1,2048,384]{2,1,0:T(8,128)S(1)}, f32[1,2048,384]{2,1,0:T(8,128)}, u32[]{:S(2)}) copy-start(f32[1,2048,384]{2,1,0:T(8,128)} %velocity.3) | copy-start | bytes 9437188
  1.7 5.3 %copy-start.3 = (f32[1,2048,128]{2,1,0:T(8,128)S(1)}, f32[1,2048,128]{2,1,0:T(8,128)}, u32[]{:S(2)}) copy-start(f32[1,2048,128]{2,1,0:T(8,128)} %inv_mass.3) | copy-start | bytes 3145732
  1.7 10.4 %collective-permute-start.1 = (f32[8,1408]{1,0:T(8,128)S(1)}, f32[8,1408]{1,0:T(8,128)S(1)}, u32[]{:S(2)}, u32[]{:S(2)}) collective-permute-start(f32[8,1408]{1,0:T(8,128)S(1)} %get-tuple-element.39), channel_id=1, source_target_pairs={{1,2},{2,1},{3,4},{4,3},{5,6},{6,5},{7,8},{8,7},{9,10},{10,9},{11,... | collective-permute-start | bytes 135176 | tf_op jit(solution)/shard_map/ppermute | solution.py:521
  6.9 5.2 %collective-permute-start = (f32[8,1408]{1,0:T(8,128)S(1)}, f32[8,1408]{1,0:T(8,128)S(1)}, u32[]{:S(2)}, u32[]{:S(2)}) collective-permute-start(f32[8,1408]{1,0:T(8,128)S(1)} %get-tuple-element.38), channel_id=1, source_target_pairs={{0,1},{1,0},{2,3},{3,2},{4,5},{5,4},{6,7},{7,6},{8,9},{9,8},{10,11... | collective-permute-start | bytes 135176 | tf_op jit(solution)/shard_map/ppermute | solution.py:533
  7.1 5.1 %copy-start.6 = (s32[1,1,3,1536]{3,1,2,0:T(1,128)S(1)}, s32[1,1,3,1536]{3,1,2,0:T(1,128)}, u32[]{:S(2)}) copy-start(s32[1,1,3,1536]{3,1,2,0:T(1,128)} %param.14) | copy-start | bytes 55300
  12.2 10.6 %copy-start.7 = (f32[1,1,3,1536]{3,1,2,0:T(1,128)S(1)}, f32[1,1,3,1536]{3,1,2,0:T(1,128)}, u32[]{:S(2)}) copy-start(f32[1,1,3,1536]{3,1,2,0:T(1,128)} %param.15) | copy-start | bytes 55300
  14.0 10.1 %collective-permute-start.2 = (f32[5,1,1536]{2,1,0:T(1,128)S(1)}, f32[5,1,1536]{2,1,0:T(1,128)S(1)}, u32[]{:S(2)}, u32[]{:S(2)}) collective-permute-start(f32[5,1,1536]{2,1,0:T(1,128)S(1)} %get-tuple-element.48), channel_id=1, source_target_pairs={{1,66},{2,65},{3,68},{4,67},{5,70},{6,69},{7,72},{8,71},{9,74},{10... | collective-permute-start | bytes 92168 | tf_op jit(solution)/shard_map/ppermute | solution.py:563
  17.9 4.9 %collective-permute-start.3 = (f32[4,1,1536]{2,1,0:T(1,128)S(1)}, f32[4,1,1536]{2,1,0:T(1,128)S(1)}, u32[]{:S(2)}, u32[]{:S(2)}) collective-permute-start(f32[4,1,1536]{2,1,0:T(1,128)S(1)} %get-tuple-element.51), channel_id=1, source_target_pairs={{0,64},{1,65},{2,66},{3,67},{4,68},{5,69},{6,70},{7,71},{8,72},{9,... | collective-permute-start | bytes 73736 | tf_op jit(solution)/shard_map/ppermute | solution.py:563
  19.6 3.2 %collective-permute-start.4 = (f32[3,1,1536]{2,1,0:T(1,128)S(1)}, f32[3,1,1536]{2,1,0:T(1,128)S(1)}, u32[]{:S(2)}, u32[]{:S(2)}) collective-permute-start(f32[3,1,1536]{2,1,0:T(1,128)S(1)} %get-tuple-element.52), channel_id=1, source_target_pairs={{0,65},{1,64},{2,67},{3,66},{4,69},{5,68},{6,71},{7,70},{8,73},{9,... | collective-permute-start | bytes 55304 | tf_op jit(solution)/shard_map/ppermute | solution.py:563

commit v3 on v2

--- a/solution.py
+++ b/solution.py
@@ -282,17 +282,54 @@
     pick_slots(points[near_offset()], table, send_near)
 
 
+def slot_weight(j, weights):
+    neighbour = lax.axis_index("patch") + (j - 1)
+    present = jnp.where((neighbour >= 0) & (neighbour < lax.axis_size("patch")), 1.0, 0.0)
+    return weights[j] * present
+
+
+def own_kernel(points, weights, compact, own, total):
+    place = lax.broadcasted_iota(jnp.int32, (128, SLOTS), 0)
+    line = lax.broadcasted_iota(jnp.int32, (16, SLOTS), 0)
+    summed = None
+    for j in range(3):
+        group_of, low, point = slot_place(points[j])
+        weight = slot_weight(j, weights)
+        upper = weight.astype(BF16).astype(F32)
+        both = jnp.where(line == point, upper, jnp.where(line == point + 8, weight - upper, 0.0)).astype(BF16)
+        zero = jnp.zeros((16, SLOTS), BF16)
+        right = jnp.concatenate([jnp.where(group_of == group, both, zero) for group in range(16)], axis=0)
+        part = dot_nt(jnp.where(place == low, 1.0, 0.0).astype(BF16), right)
+        summed = part if summed is None else summed + part
+    total[...] = summed
+    lane = lax.broadcasted_iota(jnp.int32, (128, 128), 1)
+    for group in range(16):
+        half = total[:, (group // 8) * 128 : (group // 8) * 128 + 128]
+        half = half + pltpu.roll(half, 120, 1)
+        shift = (group % 8) * 16
+        weight_sum = jnp.where(
+            lane < 3,
+            pltpu.roll(half, 128 - shift, 1) if shift else half,
+            jnp.where(
+                lane < 6,
+                pltpu.roll(half, (131 - shift) % 128, 1),
+                pltpu.roll(half, (134 - shift) % 128, 1),
+            ),
+        )
+        start = TOP + HALO + group * 128
+        own[group * 128 : group * 128 + 128, :] = jnp.where(
+            lane < 9, compact[start : start + 128, :] * weight_sum, 0.0
+        )
+
+
 def sum_slots(j, got, points, weights):
     place = lax.broadcasted_iota(jnp.int32, (128, SLOTS), 0)
     line = lax.broadcasted_iota(jnp.int32, (16, SLOTS), 0)
     group_of, low, point = slot_place(points[j])
-    neighbour = lax.axis_index("patch") + (j - 1)
-    present = jnp.where((neighbour >= 0) & (neighbour < lax.axis_size("patch")), 1.0, 0.0)
-    weight = weights[j] * present
+    weight = slot_weight(j, weights)
     spread_out = jnp.zeros((16, SLOTS), F32)
-    for c in range(4):
-        value = weight * got[c] if c < 3 else weight
-        spread_out = jnp.where(line == 3 * c + point, value, spread_out)
+    for c in range(3):
+        spread_out = jnp.where(line == 3 * c + point, weight * got[c], spread_out)
     high = spread_out.astype(BF16)
     rest = (spread_out - high.astype(F32)).astype(BF16)
     zero = jnp.zeros((16, SLOTS), BF16)
@@ -311,7 +348,7 @@
     most[...] = jnp.maximum(stiffest[...], jnp.broadcast_to(got_mid[3][:, 0:128], (8, 128)))
 
 
-def couple_kernel(got_far, points, weights, partial, most, compact, coupling, parcel, total):
+def couple_kernel(got_far, points, weights, partial, most, own, coupling, parcel, total):
     block = lax.axis_index("patch")
     blocks = lax.axis_size("patch")
     total[...] = partial[...] + sum_slots(2 - near_offset(), got_far, points, weights)
@@ -321,14 +358,8 @@
         half = total[:, (group // 8) * 128 : (group // 8) * 128 + 128]
         shift = (group % 8) * 16
         block_sum = pltpu.roll(half, 128 - shift, 1) if shift else half
-        weight_sum = jnp.where(
-            lane < 3,
-            pltpu.roll(block_sum, 119, 1),
-            jnp.where(lane < 6, pltpu.roll(block_sum, 122, 1), pltpu.roll(block_sum, 125, 1)),
-        )
         start = TOP + HALO + group * 128
-        here = block_sum - compact[start : start + 128, :] * weight_sum
-        here = jnp.where(lane < 9, here, 0.0)
+        here = jnp.where(lane < 9, block_sum, 0.0) - own[group * 128 : group * 128 + 128, :]
         coupling[start : start + 128, :] = here
         if group == 0:
             edges.append(here[0:8, :])
@@ -576,6 +607,15 @@
     )(*near(table, points, stiffest))
     got_mid = across(send_mid, mid_pairs)
     got_near = across(send_near, near_pairs)
+    own = pl.pallas_call(
+        own_kernel,
+        out_shape=pltpu.VMEM((ROWS, 128), F32),
+        in_specs=[IN_VMEM] * 3,
+        out_specs=IN_VMEM,
+        scratch_shapes=[pltpu.VMEM((128, 256), F32)],
+        compiler_params=params(12),
+        name="own",
+    )(*near(points, weights, compact))
     partial, most = pl.pallas_call(
         half_couple_kernel,
         out_shape=(pltpu.VMEM((128, 256), F32), tile),
@@ -593,7 +633,7 @@
         scratch_shapes=[pltpu.VMEM((128, 256), F32)],
         compiler_params=params(12),
         name="couple",
-    )(*near(got_far, points, weights, partial, most, compact))
+    )(*near(got_far, points, weights, partial, most, own))
     parcel = lax.all_to_all(parcel, "patch", 0, 0)
 
     new_field, new_moving, unused = pl.pallas_call(

time: 62.4 us -> 61.8 us (level)
  waiting for transfers between devices: 3.19 us -> 1.01 us
  Pallas kernels: 28.7 us -> 29.6 us
  blocking collectives: 20.3 us -> 21 us
    ppermute x3, waiting for transfers between devices: 3.19 us -> 1 us  [across(): lax.ppermute(send, both, [(g * blocks + i, (1 - g) * blocks + t) for g in...]
    pallas_call x0 -> x1, Pallas kernels: none -> 2.18 us  [per_device(): pl.pallas_call(own_kernel, out_shape=pltpu.VMEM((ROWS, 128), F32), in_spe...]
    pallas_call x1, Pallas kernels: 2.13 us -> 1 us  [per_device(): pl.pallas_call(couple_kernel, out_shape=(plane, pltpu.VMEM((blocks, 1, 12...]
    all_to_all x1, blocking collectives: 20.3 us -> 21 us  [per_device(): parcel = lax.all_to_all(parcel, 'patch', 0, 0)]
  transfers between devices with their start and end apart: 5 -> 5, of which waited for: 1 -> 1; matrix products, arithmetic and copies ran while one was open for 0% -> 0% of each run, Pallas kernels for 13% -> 17%
where the time goes in v3:
time: 61.8 us; the launch traced here: 61.6 us
  Pallas kernels  29.6 us (48%)
  blocking collectives  21 us (34%)
  starting transfers between devices  8.93 us (14%)
  between operations  1.02 us (2%)
  waiting for transfers between devices  1.01 us (2%)
    all_to_all x1, blocking collectives, per_device(): parcel = lax.all_to_all(parcel, 'patch', 0, 0)  21 us
    pallas_call x1, Pallas kernels, per_device(): pl.pallas_call(step_kernel, out_shape=(jax.ShapeDtypeStruct((1, ROWS, ROW...  15.4 us
    pallas_call x1, Pallas kernels, per_device(): pl.pallas_call(force_kernel, out_shape=(PLANE_3, PLANE_3, PLANE_1, PLANE_...  5.08 us
    ppermute x3, starting transfers between devices, across(): lax.ppermute(send, both, [(g * blocks + i, (1 - g) * blocks + t) for g in...  4.82 us
    ppermute x1, starting transfers between devices, per_device(): far_rows = lax.ppermute(far_rows, 'patch', far_pairs)  4.03 us
    pallas_call x1, Pallas kernels, per_device(): pl.pallas_call(own_kernel, out_shape=pltpu.VMEM((ROWS, 128), F32), in_spe...  2.18 us
    pallas_call x1, Pallas kernels, per_device(): pl.pallas_call(ends_kernel, out_shape=(PLANE_3, OPERAND, PLANE_3, PLANE_3...  1.76 us
    pallas_call x1, Pallas kernels, per_device(): pl.pallas_call(half_couple_kernel, out_shape=(pltpu.VMEM((128, 256), F32)...  1.27 us
  transfers between devices with their start and end apart: 5, of which 1 were waited for; matrix products, arithmetic and copies ran while one was open for 0% of the time, Pallas kernels for 17%

profile of v3, /device:TPU:33, one launch (start us, length us, event | category | flops | bytes accessed | tf_op | source)
XLA Modules:
  0.0 61.6 jit_solution(8060450619316152636)
XLA Ops:
  0.7 1.0 %bundle.1 = (f32[8,1408]{1,0:T(8,128)S(1)}, f32[8,1408]{1,0:T(8,128)S(1)}) custom-call(f32[1,2048,384]{2,1,0:T(8,128)} %displace.3, f32[1,2048,384]{2,1,0:T(8,128)} %velocity.3, f32[1,2048,384]{2,1,0:T(8,128)} %ext_force.3, f32[1,2048,128]{2,1,0:T(8,128)} %inv_mass.3, f32[1,2048,128]{2,1,0:T(8,128)} %thickness.3), custom_call_target="tpu_custom_call" | custom-call | tf_op jit(solution)/shard_map/bundle/pallas_call | solution.py:543
  1.7 0.0 copy-start
  1.7 0.0 copy-start.3
  1.7 4.0 %collective-permute-start.1 = (f32[8,1408]{1,0:T(8,128)S(1)}, f32[8,1408]{1,0:T(8,128)S(1)}, u32[]{:S(2)}, u32[]{:S(2)}) collective-permute-start(f32[8,1408]{1,0:T(8,128)S(1)} %get-tuple-element.39), channel_id=1, source_target_pairs={{1,2},{2,1},{3,4},{4,3},{5,6},{6,5},{7,8},{8,7},{9,10},{10,9},{11,... | collective-permute-start | bytes 135176 | tf_op jit(solution)/shard_map/ppermute | solution.py:552
  5.8 1.1 %load.1 = (f32[3,2080,128]{2,1,0:T(8,128)S(1)}, bf16[2,1072,384]{2,1,0:T(8,128)(2,1)S(1)}, bf16[1920,256]{1,0:T(8,128)(2,1)S(1)}, bf16[2304,256]{1,0:T(8,128)(2,...) custom-call(f32[1,2048,384]{2,1,0:T(8,128)S(1)} %copy-done.2, ...), custom_call_target="tpu_custom_call", output_to_operand_aliasing={{5}: (2, {})} | custom-call | tf_op jit(solution)/shard_map/load/pallas_call | solution.py:554
  6.9 0.1 collective-permute-start
  7.1 0.0 copy-start.6
  7.1 5.1 %force.1 = (f32[3,2080,128]{2,1,0:T(8,128)S(1)}, f32[3,2080,128]{2,1,0:T(8,128)S(1)}, f32[1,2080,128]{2,1,0:T(8,128)S(1)}, f32[1,2080,128]{2,1,0:T(8,128)S(1)}, ...) custom-call(f32[3,2080,128]{2,1,0:T(8,128)S(1)} %get-tuple-element.40.field.field_in, ...), custom_call_target="tpu_custom_call" | custom-call | tf_op jit(solution)/shard_map/force/pallas_call | solution.py:568
  12.2 0.0 collective-permute-done.1.far_rows
  12.2 0.0 collective-permute-done.near_rows
  12.2 0.0 copy-start.7
  12.2 1.8 %ends.1 = (f32[3,2080,128]{2,1,0:T(8,128)S(1)}, bf16[2,1072,384]{2,1,0:T(8,128)(2,1)S(1)}, f32[3,2080,128]{2,1,0:T(8,128)S(1)}, f32[3,2080,128]{2,1,0:T(8,128)S(...) custom-call(bf16[1920,256]{1,0:T(8,128)(2,1)S(1)} %get-tuple-element, ...), custom_call_target="tpu_custom_call", output_to_operand_aliasing={{0}: (6, {}), {1}: (7, {}), {2}: (8, {}), {3}: (9, {}), {4}... | custom-call | tf_op jit(solution)/shard_map/ends/pallas_call | solution.py:580
  14.0 3.1 %collective-permute-start.2 = (f32[5,1,1536]{2,1,0:T(1,128)S(1)}, f32[5,1,1536]{2,1,0:T(1,128)S(1)}, u32[]{:S(2)}, u32[]{:S(2)}) collective-permute-start(f32[5,1,1536]{2,1,0:T(1,128)S(1)} %get-tuple-element.48), channel_id=1, source_target_pairs={{1,66},{2,65},{3,68},{4,67},{5,70},{6,69},{7,72},{8,71},{9,74},{10... | collective-permute-start | bytes 92168 | tf_op jit(solution)/shard_map/ppermute | solution.py:594
  17.1 0.8 %pick.1 = (f32[4,1,1536]{2,1,0:T(1,128)S(1)}, f32[3,1,1536]{2,1,0:T(1,128)S(1)}) custom-call(bf16[256,256]{1,0:T(8,128)(2,1)S(1)} %get-tuple-element.49.table, s32[3,1,1536]{2,1,0:T(1,128)S(1)} %bitcast.3, f32[8,128]{1,0:T(8,128)S(1)} %get-tuple-element.50.stiffest), custom_call_target="tpu_custom_call" | custom-call | flops 1 | bytes 1 | tf_op jit(solution)/shard_map/pick/pallas_call | solution.py:599
  17.9 1.7 %collective-permute-start.3 = (f32[4,1,1536]{2,1,0:T(1,128)S(1)}, f32[4,1,1536]{2,1,0:T(1,128)S(1)}, u32[]{:S(2)}, u32[]{:S(2)}) collective-permute-start(f32[4,1,1536]{2,1,0:T(1,128)S(1)} %get-tuple-element.51), channel_id=1, source_target_pairs={{0,64},{1,65},{2,66},{3,67},{4,68},{5,69},{6,70},{7,71},{8,72},{9,... | collective-permute-start | bytes 73736 | tf_op jit(solution)/shard_map/ppermute | solution.py:594
  19.6 0.0 collective-permute-start.4
  19.6 2.2 %own.1 = f32[2048,128]{1,0:T(8,128)S(1)} custom-call(s32[3,1,1536]{2,1,0:T(1,128)S(1)} %bitcast.4, f32[3,1,1536]{2,1,0:T(1,128)S(1)} %bitcast.7, f32[2080,128]{1,0:T(8,128)S(1)} %get-tuple-element.55.compact), custom_call_target="tpu_custom_call" | custom-call | tf_op jit(solution)/shard_map/own/pallas_call | solution.py:610
  21.8 1.0 %collective-permute-done.4.got_near = f32[3,1,1536]{2,1,0:T(1,128)S(1)} collective-permute-done((f32[3,1,1536]{2,1,0:T(1,128)S(1)}, f32[3,1,1536]{2,1,0:T(1,128)S(1)}, u32[]{:S(2)}, u32[]{:S(2)}) %collective-permute-start.4) | collective-permute-done | bytes 18464 | tf_op jit(solution)/shard_map/ppermute | solution.py:594
  22.8 0.0 collective-permute-done.3.got_mid
  22.8 1.3 %half_couple.1 = (f32[128,256]{1,0:T(8,128)S(1)}, f32[8,128]{1,0:T(8,128)S(1)}) custom-call(f32[4,1,1536]{2,1,0:T(1,128)S(1)} %collective-permute-done.3.got_mid, f32[3,1,1536]{2,1,0:T(1,128)S(1)} %collective-permute-done.4.got_near, s32[3,1,1536]{2,1,0:T(1,128)S(1)} %bitcast.5, f32[3,1,1536]{2,1,0:T(1,128)S(1)} %bitcast.8, ...), custom_call_target="tpu_custom_call" | custom-call | flops 1 | bytes 1 | tf_op jit(solution)/shard_map/half_couple/pallas_call | solution.py:619
  24.1 0.0 collective-permute-done.2.got_far
  24.1 1.0 %couple.1 = (f32[2080,128]{1,0:T(8,128)S(1)}, f32[64,1,128]{2,1,0:T(1,128)S(1)}) custom-call(f32[5,1,1536]{2,1,0:T(1,128)S(1)} %collective-permute-done.2.got_far, s32[3,1,1536]{2,1,0:T(1,128)S(1)} %bitcast.6, f32[3,1,1536]{2,1,0:T(1,128)S(1)} %bitcast.9, f32[128,256]{1,0:T(8,128)S(1)} %get-tuple-element.53.partial, f32[8,128]{1,0:T(8,128)S(1)} %get-tuple-element.54.most, ...), custom_call_target="tpu_custom_call" | custom-call | tf_op jit(solution)/shard_map/couple/pallas_call | solution.py:628
  25.1 21.0 %all_to_all.5.parcel = f32[64,1,128]{2,1,0:T(1,128)S(1)} all-to-all(f32[64,1,128]{2,1,0:T(1,128)S(1)} %get-tuple-element.56), channel_id=1, replica_groups=mesh['grp'=2,'patch'=64] {'patch'}, dimensions={0} | all-to-all | bytes 65536 | tf_op jit(solution)/shard_map/all_to_all | solution.py:637
  46.1 15.4 %steps.1 = (f32[1,2048,384]{2,1,0:T(8,128)}, f32[1,2048,384]{2,1,0:T(8,128)}, f32[2080,128]{1,0:T(8,128)S(1)}) custom-call(f32[64,1,128]{2,1,0:T(1,128)S(1)} %all_to_all.5.parcel, f32[3,2080,128]{2,1,0:T(8,128)S(1)} %get-tuple-element.57.field, f32[3,2080,128]{2,1,0:T(8,128)S(1)} %get-tuple-element.58.moving, ...), custom_call_target="tpu_custom_call", output_to_operand_aliasing={{2}: (7, {})} | custom-call | tf_op jit(solution)/shard_map/steps/pallas_call | solution.py:639
  (12 shorter events, 0.0 us)
Async XLA Ops:
  0.6 5.1 %copy-start.2 = (f32[1,2048,384]{2,1,0:T(8,128)S(1)}, f32[1,2048,384]{2,1,0:T(8,128)}, u32[]{:S(2)}) copy-start(f32[1,2048,384]{2,1,0:T(8,128)} %displace.3) | copy-start | bytes 9437188
  0.6 5.1 %copy-start.5 = (bf16[5,384,384]{2,1,0:T(8,128)(2,1)S(1)}, bf16[5,384,384]{2,1,0:T(8,128)(2,1)}, u32[]{:S(2)}) copy-start(bf16[5,384,384]{2,1,0:T(8,128)(2,1)} %stiff.1) | copy-start | bytes 4423684
  0.7 6.4 %copy-start.1 = (f32[1,2048,384]{2,1,0:T(8,128)S(1)}, f32[1,2048,384]{2,1,0:T(8,128)}, u32[]{:S(2)}) copy-start(f32[1,2048,384]{2,1,0:T(8,128)} %ext_force.3) | copy-start | bytes 9437188
  0.7 6.4 %copy-start.4 = (f32[1,2048,128]{2,1,0:T(8,128)S(1)}, f32[1,2048,128]{2,1,0:T(8,128)}, u32[]{:S(2)}) copy-start(f32[1,2048,128]{2,1,0:T(8,128)} %thickness.3) | copy-start | bytes 3145732
  1.7 5.3 %copy-start = (f32[1,2048,384]{2,1,0:T(8,128)S(1)}, f32[1,2048,384]{2,1,0:T(8,128)}, u32[]{:S(2)}) copy-start(f32[1,2048,384]{2,1,0:T(8,128)} %velocity.3) | copy-start | bytes 9437188
  1.7 5.3 %copy-start.3 = (f32[1,2048,128]{2,1,0:T(8,128)S(1)}, f32[1,2048,128]{2,1,0:T(8,128)}, u32[]{:S(2)}) copy-start(f32[1,2048,128]{2,1,0:T(8,128)} %inv_mass.3) | copy-start | bytes 3145732
  1.7 10.4 %collective-permute-start.1 = (f32[8,1408]{1,0:T(8,128)S(1)}, f32[8,1408]{1,0:T(8,128)S(1)}, u32[]{:S(2)}, u32[]{:S(2)}) collective-permute-start(f32[8,1408]{1,0:T(8,128)S(1)} %get-tuple-element.39), channel_id=1, source_target_pairs={{1,2},{2,1},{3,4},{4,3},{5,6},{6,5},{7,8},{8,7},{9,10},{10,9},{11,... | collective-permute-start | bytes 135176 | tf_op jit(solution)/shard_map/ppermute | solution.py:552
  6.9 5.2 %collective-permute-start = (f32[8,1408]{1,0:T(8,128)S(1)}, f32[8,1408]{1,0:T(8,128)S(1)}, u32[]{:S(2)}, u32[]{:S(2)}) collective-permute-start(f32[8,1408]{1,0:T(8,128)S(1)} %get-tuple-element.38), channel_id=1, source_target_pairs={{0,1},{1,0},{2,3},{3,2},{4,5},{5,4},{6,7},{7,6},{8,9},{9,8},{10,11... | collective-permute-start | bytes 135176 | tf_op jit(solution)/shard_map/ppermute | solution.py:564
  7.1 5.1 %copy-start.6 = (s32[1,1,3,1536]{3,1,2,0:T(1,128)S(1)}, s32[1,1,3,1536]{3,1,2,0:T(1,128)}, u32[]{:S(2)}) copy-start(s32[1,1,3,1536]{3,1,2,0:T(1,128)} %param.14) | copy-start | bytes 55300
  12.2 7.4 %copy-start.7 = (f32[1,1,3,1536]{3,1,2,0:T(1,128)S(1)}, f32[1,1,3,1536]{3,1,2,0:T(1,128)}, u32[]{:S(2)}) copy-start(f32[1,1,3,1536]{3,1,2,0:T(1,128)} %param.15) | copy-start | bytes 55300
  14.0 10.1 %collective-permute-start.2 = (f32[5,1,1536]{2,1,0:T(1,128)S(1)}, f32[5,1,1536]{2,1,0:T(1,128)S(1)}, u32[]{:S(2)}, u32[]{:S(2)}) collective-permute-start(f32[5,1,1536]{2,1,0:T(1,128)S(1)} %get-tuple-element.48), channel_id=1, source_target_pairs={{1,66},{2,65},{3,68},{4,67},{5,70},{6,69},{7,72},{8,71},{9,74},{10... | collective-permute-start | bytes 92168 | tf_op jit(solution)/shard_map/ppermute | solution.py:594
  17.9 4.9 %collective-permute-start.3 = (f32[4,1,1536]{2,1,0:T(1,128)S(1)}, f32[4,1,1536]{2,1,0:T(1,128)S(1)}, u32[]{:S(2)}, u32[]{:S(2)}) collective-permute-start(f32[4,1,1536]{2,1,0:T(1,128)S(1)} %get-tuple-element.51), channel_id=1, source_target_pairs={{0,64},{1,65},{2,66},{3,67},{4,68},{5,69},{6,70},{7,71},{8,72},{9,... | collective-permute-start | bytes 73736 | tf_op jit(solution)/shard_map/ppermute | solution.py:594
  19.6 3.2 %collective-permute-start.4 = (f32[3,1,1536]{2,1,0:T(1,128)S(1)}, f32[3,1,1536]{2,1,0:T(1,128)S(1)}, u32[]{:S(2)}, u32[]{:S(2)}) collective-permute-start(f32[3,1,1536]{2,1,0:T(1,128)S(1)} %get-tuple-element.52), channel_id=1, source_target_pairs={{0,65},{1,64},{2,67},{3,66},{4,69},{5,68},{6,71},{7,70},{8,73},{9,... | collective-permute-start | bytes 55304 | tf_op jit(solution)/shard_map/ppermute | solution.py:594

commit v4 on v3

--- a/solution.py
+++ b/solution.py
@@ -22,6 +22,7 @@
 BAND_ROWS = (PAIRS + 2) * 16
 CHUNK = 208
 CHUNK_PAIRS = CHUNK // 16
+EARLY = 4 * CHUNK_PAIRS
 F32 = jnp.float32
 BF16 = jnp.bfloat16
 
@@ -161,13 +162,22 @@
         )
 
 
+def turn_rows(compact, table, groups):
+    for group in groups:
+        start = TOP + HALO + group * 128
+        turned = compact[start : start + 128, :].T[0:16, :]
+        upper = turned.astype(BF16)
+        table[group * 16 : group * 16 + 16, 0:128] = upper
+        table[group * 16 : group * 16 + 16, 128:256] = (turned - upper.astype(F32)).astype(BF16)
+
+
 def some_rows(results, i):
     return [[part[i * 16 : i * 16 + 16, :] for part in half] for half in results]
 
 
 def force_kernel(
     field, operand, wide_a, wide_b, wide_c, velocity, ext_force, inv_mass, thickness,
-    moving, outer, mass, thick, force, compact, stiffest,
+    moving, outer, mass, thick, force, compact, stiffest, table,
     sem_moving, sem_outer, sem_mass, sem_thick,
 ):
     thick_in = plane_copies(thickness, thick, 1, sem_thick)
@@ -204,6 +214,7 @@
     most = jnp.max(jnp.max(product, axis=0, keepdims=True), axis=1, keepdims=True)
     stiffest[...] = jnp.broadcast_to(most, (8, 128))
     make_compact(*before)
+    turn_rows(compact, table, range(1, 15))
     for copy in outer_in:
         copy.wait()
 
@@ -235,7 +246,7 @@
 
 def ends_kernel(
     wide_a, wide_b, wide_c, near_rows, far_rows, points,
-    field_in, operand_in, moving_in, outer_in, mass_in, thick_in, force_in, compact_in,
+    field_in, operand_in, moving_in, outer_in, mass_in, thick_in, force_in, compact_in, table_in,
     field, operand, moving, outer, mass, thick, force, compact, table, send_far,
 ):
     even = lax.axis_index("patch") % 2 == 0
@@ -265,12 +276,7 @@
             force[half, HIGH_PAIR * 16 : PAIR_ROWS, cols(c)] = results[half][c][low:]
     for i, step in enumerate(list(range(LOW_PAIRS)) + list(range(HIGH_PAIR, PAIRS))):
         compact_rows(step, field, moving, thick, compact, some_rows(results, i))
-    for group in range(16):
-        start = TOP + HALO + group * 128
-        turned = compact[start : start + 128, :].T[0:16, :]
-        upper = turned.astype(BF16)
-        table[group * 16 : group * 16 + 16, 0:128] = upper
-        table[group * 16 : group * 16 + 16, 128:256] = (turned - upper.astype(F32)).astype(BF16)
+    turn_rows(compact, table, [0, 15])
     pick_slots(points[2 - near_offset()], table, send_far)
     for c in range(3, FAR_ROWS):
         send_far[c] = jnp.zeros((1, SLOTS), F32)
@@ -379,7 +385,7 @@
 def step_kernel(
     parcel, field, moving, outer, mass, thick, force, coupling_in, wide_a, wide_b, wide_c,
     new_field, new_moving, couple,
-    state, speed, push, drag, operand_a, operand_b, place_out, speed_out, sem_out,
+    state, speed, push, drag, operand_a, operand_b, place_out, speed_out, place_late, speed_late, sem_out, sem_late,
 ):
     block = lax.axis_index("patch")
     blocks = lax.axis_size("patch")
@@ -438,6 +444,19 @@
             return carry
 
         lax.fori_loop(0, PAIRS // 5, some, 0)
+        out = []
+        for c in range(3):
+            inner = pl.ds(TOP + HALO, ROWS)
+            out.append(
+                pltpu.make_async_copy(place_out.at[c, inner, :], new_field.at[0, :, pl.ds(c * 128, 128)], sem_out.at[c])
+            )
+            out.append(
+                pltpu.make_async_copy(speed_out.at[c, inner, :], new_moving.at[0, :, pl.ds(c * 128, 128)], sem_out.at[3 + c])
+            )
+        for copy in out:
+            copy.start()
+        for copy in out:
+            copy.wait()
 
     def low_ends(operand):
         for c in range(3):
@@ -463,9 +482,15 @@
                     following[half, start + 16 : start + 16 + CHUNK, cols(c)] = place.astype(BF16)
                 else:
                     for i in range(CHUNK_PAIRS):
-                        at = spread(2 * (start // 16 + i) + half)
-                        place_out[c, at, :] = place[i * 16 : i * 16 + 16, :]
-                        speed_out[c, at, :] = new_speed[i * 16 : i * 16 + 16, :] * inverse
+                        k = 2 * (start // 16 + i) + half
+                        some_place = place[i * 16 : i * 16 + 16, :]
+                        some_speed = new_speed[i * 16 : i * 16 + 16, :] * inverse
+                        if k >= EARLY:
+                            place_out[c, spread(k), :] = some_place
+                            speed_out[c, spread(k), :] = some_speed
+                        if k < EARLY + 8 or RUN - 9 <= k < RUN:
+                            place_late[c, spread(k), :] = some_place
+                            speed_late[c, spread(k), :] = some_speed
         if following is not None and chunk == 0:
             high_ends(following)
         if following is not None and chunk == PAIR_ROWS // CHUNK - 1:
@@ -477,6 +502,32 @@
             first_update(step, True)
         low_ends(operand_a)
         high_ends(operand_a)
+        pieces = []
+        done = 0
+        for run in range(16):
+            begin = (run * RUN + EARLY - HALO + 7) // 8 * 8
+            end = min((run * RUN + RUN - HALO) // 8 * 8, ROWS)
+            pieces.append((done, begin, end))
+            done = end
+        assert done == ROWS
+        targets = [(place_out, place_late, new_field), (speed_out, speed_late, new_moving)]
+
+        def copies(late, rows):
+            made = []
+            for i, pair in enumerate(targets):
+                for c in range(3):
+                    for first, count in rows:
+                        made.append(
+                            pltpu.make_async_copy(
+                                pair[late].at[c, pl.ds(TOP + HALO + first, count), :],
+                                pair[2].at[0, pl.ds(first, count), pl.ds(c * 128, 128)],
+                                (sem_late if late else sem_out).at[3 * i + c],
+                            )
+                        )
+            return made
+
+        early_rows = [(begin, end - begin) for _, begin, end in pieces]
+        late_rows = [(gap, begin - gap) for gap, begin, _ in pieces]
         before = None
         for operand, following, order in [
             (operand_a, operand_b, [0, 1, 2, 3, 4]),
@@ -491,22 +542,16 @@
                         first_update(step, True)
                 if before is not None:
                     update(*before)
+                    if before[0] == 4 and before[2] is None:
+                        for copy in copies(0, early_rows):
+                            copy.start()
                 before = (chunk, results, following)
         update(*before)
-
-    out = []
-    for c in range(3):
-        inner = pl.ds(TOP + HALO, ROWS)
-        out.append(
-            pltpu.make_async_copy(place_out.at[c, inner, :], new_field.at[0, :, pl.ds(c * 128, 128)], sem_out.at[c])
-        )
-        out.append(
-            pltpu.make_async_copy(speed_out.at[c, inner, :], new_moving.at[0, :, pl.ds(c * 128, 128)], sem_out.at[3 + c])
-        )
-    for copy in out:
-        copy.start()
-    for copy in out:
-        copy.wait()
+        for copy in copies(1, late_rows):
+            copy.start()
+        for late, rows in enumerate([early_rows, late_rows]):
+            for copy in copies(late, [(0, sum(count for _, count in rows))]):
+                copy.wait()
 
 
 ANY = pl.BlockSpec(memory_space=pl.ANY)
@@ -565,27 +610,27 @@
 
     plane = pltpu.VMEM((PLANE, 128), F32)
     tile = pltpu.VMEM((8, 128), F32)
-    moving, outer, mass, thick, force, compact, stiffest = pl.pallas_call(
+    table = pltpu.VMEM((256, 256), BF16)
+    moving, outer, mass, thick, force, compact, stiffest, turned = pl.pallas_call(
         force_kernel,
-        out_shape=(PLANE_3, PLANE_3, PLANE_1, PLANE_1, FULL, plane, tile),
+        out_shape=(PLANE_3, PLANE_3, PLANE_1, PLANE_1, FULL, plane, tile, table),
         in_specs=[IN_VMEM] * 5 + [ANY] * 4,
-        out_specs=[IN_VMEM] * 7,
+        out_specs=[IN_VMEM] * 8,
         scratch_shapes=[DMA((3,)), DMA((3,)), DMA((1,)), DMA((1,))],
         compiler_params=params(12),
         name="force",
     )(*near(field, operand, *bands), velocity, ext_force, inv_mass, thickness)
 
     slots = pltpu.VMEM((3, 1, SLOTS), F32)
-    table = pltpu.VMEM((256, 256), BF16)
     field, operand, moving, outer, mass, thick, force, compact, table, send_far = pl.pallas_call(
         ends_kernel,
         out_shape=(PLANE_3, OPERAND, PLANE_3, PLANE_3, PLANE_1, PLANE_1, FULL, plane, table, pltpu.VMEM((FAR_ROWS, 1, SLOTS), F32)),
-        in_specs=[IN_VMEM] * 14,
+        in_specs=[IN_VMEM] * 15,
         out_specs=[IN_VMEM] * 10,
-        input_output_aliases={i + 6: i for i in range(8)},
+        input_output_aliases={i + 6: i for i in range(9)},
         compiler_params=params(12),
         name="ends",
-    )(*near(*bands, near_rows, far_rows, points, field, operand, moving, outer, mass, thick, force, compact))
+    )(*near(*bands, near_rows, far_rows, points, field, operand, moving, outer, mass, thick, force, compact, turned))
 
     both = ("grp", "patch")
     mid_pairs = [(i, i) for i in range(blocks)]
@@ -647,8 +692,8 @@
         out_specs=[ANY] * 2 + [IN_VMEM],
         input_output_aliases={7: 2},
         scratch_shapes=[FULL, FULL, FULL, pltpu.VMEM((2, PAIR_ROWS, 128), F32)]
-        + [OPERAND, OPERAND, PLANE_3, PLANE_3, DMA((6,))],
-        compiler_params=params(28),
+        + [OPERAND, OPERAND, PLANE_3, PLANE_3, PLANE_3, PLANE_3, DMA((6,)), DMA((6,))],
+        compiler_params=params(35),
         name="steps",
     )(*near(parcel, field, moving, outer, mass, thick, force, coupling, *bands))
     return new_field, new_moving

time: 61.8 us -> 60.7 us (0.982)
  Pallas kernels: 29.6 us -> 28.5 us
    pallas_call x1, Pallas kernels: 15.4 us -> 14.3 us  [per_device(): pl.pallas_call(step_kernel, out_shape=(jax.ShapeDtypeStruct((1, ROWS, ROW...]
  transfers between devices with their start and end apart: 5 -> 5, of which waited for: 1 -> 1; matrix products, arithmetic and copies ran while one was open for 0% -> 0% of each run, Pallas kernels for 17% -> 18%
where the time goes in v4:
time: 60.7 us; the launch traced here: 60.5 us
  Pallas kernels  28.5 us (47%)
  blocking collectives  21 us (35%)
  starting transfers between devices  8.94 us (15%)
  between operations  1.02 us (2%)
  waiting for transfers between devices  1.01 us (2%)
    all_to_all x1, blocking collectives, per_device(): parcel = lax.all_to_all(parcel, 'patch', 0, 0)  21 us
    pallas_call x1, Pallas kernels, per_device(): pl.pallas_call(step_kernel, out_shape=(jax.ShapeDtypeStruct((1, ROWS, ROW...  14.3 us
    pallas_call x1, Pallas kernels, per_device(): pl.pallas_call(force_kernel, out_shape=(PLANE_3, PLANE_3, PLANE_1, PLANE_...  5.31 us
    ppermute x3, starting transfers between devices, across(): lax.ppermute(send, both, [(g * blocks + i, (1 - g) * blocks + t) for g in...  4.83 us
    ppermute x1, starting transfers between devices, per_device(): far_rows = lax.ppermute(far_rows, 'patch', far_pairs)  4.03 us
    pallas_call x1, Pallas kernels, per_device(): pl.pallas_call(own_kernel, out_shape=pltpu.VMEM((ROWS, 128), F32), in_spe...  2.17 us
    pallas_call x1, Pallas kernels, per_device(): pl.pallas_call(ends_kernel, out_shape=(PLANE_3, OPERAND, PLANE_3, PLANE_3...  1.57 us
    pallas_call x1, Pallas kernels, per_device(): pl.pallas_call(half_couple_kernel, out_shape=(pltpu.VMEM((128, 256), F32)...  1.27 us
  transfers between devices with their start and end apart: 5, of which 1 were waited for; matrix products, arithmetic and copies ran while one was open for 0% of the time, Pallas kernels for 18%

profile of v4, /device:TPU:33, one launch (start us, length us, event | category | flops | bytes accessed | tf_op | source)
XLA Modules:
  0.0 60.5 jit_solution(8157009185637980844)
XLA Ops:
  0.7 1.0 %bundle.1 = (f32[8,1408]{1,0:T(8,128)S(1)}, f32[8,1408]{1,0:T(8,128)S(1)}) custom-call(f32[1,2048,384]{2,1,0:T(8,128)} %displace.3, f32[1,2048,384]{2,1,0:T(8,128)} %velocity.3, f32[1,2048,384]{2,1,0:T(8,128)} %ext_force.3, f32[1,2048,128]{2,1,0:T(8,128)} %inv_mass.3, f32[1,2048,128]{2,1,0:T(8,128)} %thickness.3), custom_call_target="tpu_custom_call" | custom-call | tf_op jit(solution)/shard_map/bundle/pallas_call | solution.py:588
  1.7 0.0 copy-start
  1.7 0.0 copy-start.3
  1.7 4.0 %collective-permute-start.1 = (f32[8,1408]{1,0:T(8,128)S(1)}, f32[8,1408]{1,0:T(8,128)S(1)}, u32[]{:S(2)}, u32[]{:S(2)}) collective-permute-start(f32[8,1408]{1,0:T(8,128)S(1)} %get-tuple-element.40), channel_id=1, source_target_pairs={{1,2},{2,1},{3,4},{4,3},{5,6},{6,5},{7,8},{8,7},{9,10},{10,9},{11,... | collective-permute-start | bytes 135176 | tf_op jit(solution)/shard_map/ppermute | solution.py:597
  5.8 1.1 %load.1 = (f32[3,2080,128]{2,1,0:T(8,128)S(1)}, bf16[2,1072,384]{2,1,0:T(8,128)(2,1)S(1)}, bf16[1920,256]{1,0:T(8,128)(2,1)S(1)}, bf16[2304,256]{1,0:T(8,128)(2,...) custom-call(f32[1,2048,384]{2,1,0:T(8,128)S(1)} %copy-done.2, ...), custom_call_target="tpu_custom_call", output_to_operand_aliasing={{5}: (2, {})} | custom-call | tf_op jit(solution)/shard_map/load/pallas_call | solution.py:599
  6.9 0.1 collective-permute-start
  7.1 0.0 copy-start.6
  7.1 5.3 %force.1 = (f32[3,2080,128]{2,1,0:T(8,128)S(1)}, f32[3,2080,128]{2,1,0:T(8,128)S(1)}, f32[1,2080,128]{2,1,0:T(8,128)S(1)}, f32[1,2080,128]{2,1,0:T(8,128)S(1)}, ...) custom-call(f32[3,2080,128]{2,1,0:T(8,128)S(1)} %get-tuple-element.4, ...), custom_call_target="tpu_custom_call" | custom-call | tf_op jit(solution)/shard_map/force/pallas_call | solution.py:614
  12.4 0.0 collective-permute-done.1.far_rows
  12.4 0.0 collective-permute-done.near_rows
  12.4 0.0 copy-start.7
  12.4 1.6 %ends.1 = (f32[3,2080,128]{2,1,0:T(8,128)S(1)}, bf16[2,1072,384]{2,1,0:T(8,128)(2,1)S(1)}, f32[3,2080,128]{2,1,0:T(8,128)S(1)}, f32[3,2080,128]{2,1,0:T(8,128)S(...) custom-call(bf16[1920,256]{1,0:T(8,128)(2,1)S(1)} %get-tuple-element, ...), custom_call_target="tpu_custom_call", output_to_operand_aliasing={{0}: (6, {}), {1}: (7, {}), {2}: (8, {}), {3}: (9, {}), {4}... | custom-call | tf_op jit(solution)/shard_map/ends/pallas_call | solution.py:625
  14.0 3.1 %collective-permute-start.2 = (f32[5,1,1536]{2,1,0:T(1,128)S(1)}, f32[5,1,1536]{2,1,0:T(1,128)S(1)}, u32[]{:S(2)}, u32[]{:S(2)}) collective-permute-start(f32[5,1,1536]{2,1,0:T(1,128)S(1)} %get-tuple-element.50), channel_id=1, source_target_pairs={{1,66},{2,65},{3,68},{4,67},{5,70},{6,69},{7,72},{8,71},{9,74},{10... | collective-permute-start | bytes 92168 | tf_op jit(solution)/shard_map/ppermute | solution.py:639
  17.1 0.8 %pick.1 = (f32[4,1,1536]{2,1,0:T(1,128)S(1)}, f32[3,1,1536]{2,1,0:T(1,128)S(1)}) custom-call(bf16[256,256]{1,0:T(8,128)(2,1)S(1)} %get-tuple-element.51.table, s32[3,1,1536]{2,1,0:T(1,128)S(1)} %bitcast.3, f32[8,128]{1,0:T(8,128)S(1)} %get-tuple-element.52.stiffest), custom_call_target="tpu_custom_call" | custom-call | flops 1 | bytes 1 | tf_op jit(solution)/shard_map/pick/pallas_call | solution.py:644
  17.9 1.7 %collective-permute-start.3 = (f32[4,1,1536]{2,1,0:T(1,128)S(1)}, f32[4,1,1536]{2,1,0:T(1,128)S(1)}, u32[]{:S(2)}, u32[]{:S(2)}) collective-permute-start(f32[4,1,1536]{2,1,0:T(1,128)S(1)} %get-tuple-element.53), channel_id=1, source_target_pairs={{0,64},{1,65},{2,66},{3,67},{4,68},{5,69},{6,70},{7,71},{8,72},{9,... | collective-permute-start | bytes 73736 | tf_op jit(solution)/shard_map/ppermute | solution.py:639
  19.6 0.0 collective-permute-start.4
  19.6 2.2 %own.1 = f32[2048,128]{1,0:T(8,128)S(1)} custom-call(s32[3,1,1536]{2,1,0:T(1,128)S(1)} %bitcast.4, f32[3,1,1536]{2,1,0:T(1,128)S(1)} %bitcast.7, f32[2080,128]{1,0:T(8,128)S(1)} %get-tuple-element.57.compact), custom_call_target="tpu_custom_call" | custom-call | tf_op jit(solution)/shard_map/own/pallas_call | solution.py:655
  21.8 1.0 %collective-permute-done.4.got_near = f32[3,1,1536]{2,1,0:T(1,128)S(1)} collective-permute-done((f32[3,1,1536]{2,1,0:T(1,128)S(1)}, f32[3,1,1536]{2,1,0:T(1,128)S(1)}, u32[]{:S(2)}, u32[]{:S(2)}) %collective-permute-start.4) | collective-permute-done | bytes 18464 | tf_op jit(solution)/shard_map/ppermute | solution.py:639
  22.8 0.0 collective-permute-done.3.got_mid
  22.8 1.3 %half_couple.1 = (f32[128,256]{1,0:T(8,128)S(1)}, f32[8,128]{1,0:T(8,128)S(1)}) custom-call(f32[4,1,1536]{2,1,0:T(1,128)S(1)} %collective-permute-done.3.got_mid, f32[3,1,1536]{2,1,0:T(1,128)S(1)} %collective-permute-done.4.got_near, s32[3,1,1536]{2,1,0:T(1,128)S(1)} %bitcast.5, f32[3,1,1536]{2,1,0:T(1,128)S(1)} %bitcast.8, ...), custom_call_target="tpu_custom_call" | custom-call | flops 1 | bytes 1 | tf_op jit(solution)/shard_map/half_couple/pallas_call | solution.py:664
  24.1 0.0 collective-permute-done.2.got_far
  24.1 1.0 %couple.1 = (f32[2080,128]{1,0:T(8,128)S(1)}, f32[64,1,128]{2,1,0:T(1,128)S(1)}) custom-call(f32[5,1,1536]{2,1,0:T(1,128)S(1)} %collective-permute-done.2.got_far, s32[3,1,1536]{2,1,0:T(1,128)S(1)} %bitcast.6, f32[3,1,1536]{2,1,0:T(1,128)S(1)} %bitcast.9, f32[128,256]{1,0:T(8,128)S(1)} %get-tuple-element.55.partial, f32[8,128]{1,0:T(8,128)S(1)} %get-tuple-element.56.most, ...), custom_call_target="tpu_custom_call" | custom-call | tf_op jit(solution)/shard_map/couple/pallas_call | solution.py:673
  25.1 21.0 %all_to_all.5.parcel = f32[64,1,128]{2,1,0:T(1,128)S(1)} all-to-all(f32[64,1,128]{2,1,0:T(1,128)S(1)} %get-tuple-element.58), channel_id=1, replica_groups=mesh['grp'=2,'patch'=64] {'patch'}, dimensions={0} | all-to-all | bytes 65536 | tf_op jit(solution)/shard_map/all_to_all | solution.py:682
  46.1 14.3 %steps.1 = (f32[1,2048,384]{2,1,0:T(8,128)}, f32[1,2048,384]{2,1,0:T(8,128)}, f32[2080,128]{1,0:T(8,128)S(1)}) custom-call(f32[64,1,128]{2,1,0:T(1,128)S(1)} %all_to_all.5.parcel, f32[3,2080,128]{2,1,0:T(8,128)S(1)} %get-tuple-element.59.field, f32[3,2080,128]{2,1,0:T(8,128)S(1)} %get-tuple-element.60.moving, ...), custom_call_target="tpu_custom_call", output_to_operand_aliasing={{2}: (7, {})} | custom-call | tf_op jit(solution)/shard_map/steps/pallas_call | solution.py:684
  (12 shorter events, 0.0 us)
Async XLA Ops:
  0.6 5.1 %copy-start.2 = (f32[1,2048,384]{2,1,0:T(8,128)S(1)}, f32[1,2048,384]{2,1,0:T(8,128)}, u32[]{:S(2)}) copy-start(f32[1,2048,384]{2,1,0:T(8,128)} %displace.3) | copy-start | bytes 9437188
  0.6 5.1 %copy-start.5 = (bf16[5,384,384]{2,1,0:T(8,128)(2,1)S(1)}, bf16[5,384,384]{2,1,0:T(8,128)(2,1)}, u32[]{:S(2)}) copy-start(bf16[5,384,384]{2,1,0:T(8,128)(2,1)} %stiff.1) | copy-start | bytes 4423684
  0.7 6.4 %copy-start.1 = (f32[1,2048,384]{2,1,0:T(8,128)S(1)}, f32[1,2048,384]{2,1,0:T(8,128)}, u32[]{:S(2)}) copy-start(f32[1,2048,384]{2,1,0:T(8,128)} %ext_force.3) | copy-start | bytes 9437188
  0.7 6.4 %copy-start.4 = (f32[1,2048,128]{2,1,0:T(8,128)S(1)}, f32[1,2048,128]{2,1,0:T(8,128)}, u32[]{:S(2)}) copy-start(f32[1,2048,128]{2,1,0:T(8,128)} %thickness.3) | copy-start | bytes 3145732
  1.7 5.3 %copy-start = (f32[1,2048,384]{2,1,0:T(8,128)S(1)}, f32[1,2048,384]{2,1,0:T(8,128)}, u32[]{:S(2)}) copy-start(f32[1,2048,384]{2,1,0:T(8,128)} %velocity.3) | copy-start | bytes 9437188
  1.7 5.3 %copy-start.3 = (f32[1,2048,128]{2,1,0:T(8,128)S(1)}, f32[1,2048,128]{2,1,0:T(8,128)}, u32[]{:S(2)}) copy-start(f32[1,2048,128]{2,1,0:T(8,128)} %inv_mass.3) | copy-start | bytes 3145732
  1.7 10.7 %collective-permute-start.1 = (f32[8,1408]{1,0:T(8,128)S(1)}, f32[8,1408]{1,0:T(8,128)S(1)}, u32[]{:S(2)}, u32[]{:S(2)}) collective-permute-start(f32[8,1408]{1,0:T(8,128)S(1)} %get-tuple-element.40), channel_id=1, source_target_pairs={{1,2},{2,1},{3,4},{4,3},{5,6},{6,5},{7,8},{8,7},{9,10},{10,9},{11,... | collective-permute-start | bytes 135176 | tf_op jit(solution)/shard_map/ppermute | solution.py:597
  6.9 5.5 %collective-permute-start = (f32[8,1408]{1,0:T(8,128)S(1)}, f32[8,1408]{1,0:T(8,128)S(1)}, u32[]{:S(2)}, u32[]{:S(2)}) collective-permute-start(f32[8,1408]{1,0:T(8,128)S(1)} %get-tuple-element.39), channel_id=1, source_target_pairs={{0,1},{1,0},{2,3},{3,2},{4,5},{5,4},{6,7},{7,6},{8,9},{9,8},{10,11... | collective-permute-start | bytes 135176 | tf_op jit(solution)/shard_map/ppermute | solution.py:609
  7.1 5.4 %copy-start.6 = (s32[1,1,3,1536]{3,1,2,0:T(1,128)S(1)}, s32[1,1,3,1536]{3,1,2,0:T(1,128)}, u32[]{:S(2)}) copy-start(s32[1,1,3,1536]{3,1,2,0:T(1,128)} %param.14) | copy-start | bytes 55300
  12.4 7.2 %copy-start.7 = (f32[1,1,3,1536]{3,1,2,0:T(1,128)S(1)}, f32[1,1,3,1536]{3,1,2,0:T(1,128)}, u32[]{:S(2)}) copy-start(f32[1,1,3,1536]{3,1,2,0:T(1,128)} %param.15) | copy-start | bytes 55300
  14.0 10.1 %collective-permute-start.2 = (f32[5,1,1536]{2,1,0:T(1,128)S(1)}, f32[5,1,1536]{2,1,0:T(1,128)S(1)}, u32[]{:S(2)}, u32[]{:S(2)}) collective-permute-start(f32[5,1,1536]{2,1,0:T(1,128)S(1)} %get-tuple-element.50), channel_id=1, source_target_pairs={{1,66},{2,65},{3,68},{4,67},{5,70},{6,69},{7,72},{8,71},{9,74},{10... | collective-permute-start | bytes 92168 | tf_op jit(solution)/shard_map/ppermute | solution.py:639
  17.9 4.9 %collective-permute-start.3 = (f32[4,1,1536]{2,1,0:T(1,128)S(1)}, f32[4,1,1536]{2,1,0:T(1,128)S(1)}, u32[]{:S(2)}, u32[]{:S(2)}) collective-permute-start(f32[4,1,1536]{2,1,0:T(1,128)S(1)} %get-tuple-element.53), channel_id=1, source_target_pairs={{0,64},{1,65},{2,66},{3,67},{4,68},{5,69},{6,70},{7,71},{8,72},{9,... | collective-permute-start | bytes 73736 | tf_op jit(solution)/shard_map/ppermute | solution.py:639
  19.6 3.2 %collective-permute-start.4 = (f32[3,1,1536]{2,1,0:T(1,128)S(1)}, f32[3,1,1536]{2,1,0:T(1,128)S(1)}, u32[]{:S(2)}, u32[]{:S(2)}) collective-permute-start(f32[3,1,1536]{2,1,0:T(1,128)S(1)} %get-tuple-element.54), channel_id=1, source_target_pairs={{0,65},{1,64},{2,67},{3,66},{4,69},{5,68},{6,71},{7,70},{8,73},{9,... | collective-permute-start | bytes 55304 | tf_op jit(solution)/shard_map/ppermute | solution.py:639

commit v5 on v4

--- a/solution.py
+++ b/solution.py
@@ -283,9 +283,9 @@
 
 
 def pick_kernel(table, points, stiffest, send_mid, send_near):
-    send_mid[3] = jnp.concatenate([stiffest[0:1, :]] * (SLOTS // 128), axis=1)
+    send_near[3] = jnp.concatenate([stiffest[0:1, :]] * (SLOTS // 128), axis=1)
+    pick_slots(points[near_offset()], table, send_near)
     pick_slots(points[1], table, send_mid)
-    pick_slots(points[near_offset()], table, send_near)
 
 
 def slot_weight(j, weights):
@@ -351,7 +351,7 @@
 
 def half_couple_kernel(got_mid, got_near, points, weights, stiffest, partial, most):
     partial[...] = sum_slots(1, got_mid, points, weights) + sum_slots(near_offset(), got_near, points, weights)
-    most[...] = jnp.maximum(stiffest[...], jnp.broadcast_to(got_mid[3][:, 0:128], (8, 128)))
+    most[...] = jnp.maximum(stiffest[...], jnp.broadcast_to(got_near[3][:, 0:128], (8, 128)))
 
 
 def couple_kernel(got_far, points, weights, partial, most, own, coupling, parcel, total):
@@ -643,7 +643,7 @@
     got_far = across(send_far, far_pairs)
     send_mid, send_near = pl.pallas_call(
         pick_kernel,
-        out_shape=(pltpu.VMEM((4, 1, SLOTS), F32), slots),
+        out_shape=(slots, pltpu.VMEM((4, 1, SLOTS), F32)),
         in_specs=[IN_VMEM] * 3,
         out_specs=[IN_VMEM] * 2,
         compiler_params=params(12),

time: 60.7 us -> 61 us (level)
  blocking collectives: 21 us -> 22.2 us
  waiting for transfers between devices: 1.01 us -> 0.01 us
    all_to_all x1, blocking collectives: 21 us -> 22.2 us  [per_device(): parcel = lax.all_to_all(parcel, 'patch', 0, 0)]
    ppermute x3, waiting for transfers between devices: 1.01 us -> 0.01 us  [across(): lax.ppermute(send, both, [(g * blocks + i, (1 - g) * blocks + t) for g in...]
  transfers between devices with their start and end apart: 5 -> 5, of which waited for: 1 -> 0; matrix products, arithmetic and copies ran while one was open for 0% -> 0% of each run, Pallas kernels for 18% -> 18%
where the time goes in v5:
time: 61 us; the launch traced here: 60.8 us
  Pallas kernels  28.5 us (47%)
  blocking collectives  22.2 us (36%)
  starting transfers between devices  9.02 us (15%)
  between operations  1.04 us (2%)
    all_to_all x1, blocking collectives, per_device(): parcel = lax.all_to_all(parcel, 'patch', 0, 0)  22.2 us
    pallas_call x1, Pallas kernels, per_device(): pl.pallas_call(step_kernel, out_shape=(jax.ShapeDtypeStruct((1, ROWS, ROW...  14.3 us
    pallas_call x1, Pallas kernels, per_device(): pl.pallas_call(force_kernel, out_shape=(PLANE_3, PLANE_3, PLANE_1, PLANE_...  5.31 us
    ppermute x3, starting transfers between devices, across(): lax.ppermute(send, both, [(g * blocks + i, (1 - g) * blocks + t) for g in...  4.91 us
    ppermute x1, starting transfers between devices, per_device(): far_rows = lax.ppermute(far_rows, 'patch', far_pairs)  4.03 us
    pallas_call x1, Pallas kernels, per_device(): pl.pallas_call(own_kernel, out_shape=pltpu.VMEM((ROWS, 128), F32), in_spe...  2.17 us
    pallas_call x1, Pallas kernels, per_device(): pl.pallas_call(ends_kernel, out_shape=(PLANE_3, OPERAND, PLANE_3, PLANE_3...  1.57 us
    pallas_call x1, Pallas kernels, per_device(): pl.pallas_call(half_couple_kernel, out_shape=(pltpu.VMEM((128, 256), F32)...  1.27 us
  transfers between devices with their start and end apart: 5, of which 0 were waited for; matrix products, arithmetic and copies ran while one was open for 0% of the time, Pallas kernels for 18%

profile of v5, /device:TPU:33, one launch (start us, length us, event | category | flops | bytes accessed | tf_op | source)
XLA Modules:
  0.0 60.8 jit_solution(7374972031133301901)
XLA Ops:
  0.7 1.0 %bundle.1 = (f32[8,1408]{1,0:T(8,128)S(1)}, f32[8,1408]{1,0:T(8,128)S(1)}) custom-call(f32[1,2048,384]{2,1,0:T(8,128)} %displace.3, f32[1,2048,384]{2,1,0:T(8,128)} %velocity.3, f32[1,2048,384]{2,1,0:T(8,128)} %ext_force.3, f32[1,2048,128]{2,1,0:T(8,128)} %inv_mass.3, f32[1,2048,128]{2,1,0:T(8,128)} %thickness.3), custom_call_target="tpu_custom_call" | custom-call | tf_op jit(solution)/shard_map/bundle/pallas_call | solution.py:588
  1.7 0.0 copy-start
  1.7 0.0 copy-start.3
  1.7 4.0 %collective-permute-start.1 = (f32[8,1408]{1,0:T(8,128)S(1)}, f32[8,1408]{1,0:T(8,128)S(1)}, u32[]{:S(2)}, u32[]{:S(2)}) collective-permute-start(f32[8,1408]{1,0:T(8,128)S(1)} %get-tuple-element.40), channel_id=1, source_target_pairs={{1,2},{2,1},{3,4},{4,3},{5,6},{6,5},{7,8},{8,7},{9,10},{10,9},{11,... | collective-permute-start | bytes 135176 | tf_op jit(solution)/shard_map/ppermute | solution.py:597
  5.8 1.1 %load.1 = (f32[3,2080,128]{2,1,0:T(8,128)S(1)}, bf16[2,1072,384]{2,1,0:T(8,128)(2,1)S(1)}, bf16[1920,256]{1,0:T(8,128)(2,1)S(1)}, bf16[2304,256]{1,0:T(8,128)(2,...) custom-call(f32[1,2048,384]{2,1,0:T(8,128)S(1)} %copy-done.2, ...), custom_call_target="tpu_custom_call", output_to_operand_aliasing={{5}: (2, {})} | custom-call | tf_op jit(solution)/shard_map/load/pallas_call | solution.py:599
  6.9 0.1 collective-permute-start
  7.1 0.0 copy-start.6
  7.1 5.3 %force.1 = (f32[3,2080,128]{2,1,0:T(8,128)S(1)}, f32[3,2080,128]{2,1,0:T(8,128)S(1)}, f32[1,2080,128]{2,1,0:T(8,128)S(1)}, f32[1,2080,128]{2,1,0:T(8,128)S(1)}, ...) custom-call(f32[3,2080,128]{2,1,0:T(8,128)S(1)} %get-tuple-element.4, ...), custom_call_target="tpu_custom_call" | custom-call | tf_op jit(solution)/shard_map/force/pallas_call | solution.py:614
  12.4 0.0 collective-permute-done.1.far_rows
  12.4 0.0 collective-permute-done.near_rows
  12.4 0.0 copy-start.7
  12.4 1.6 %ends.1 = (f32[3,2080,128]{2,1,0:T(8,128)S(1)}, bf16[2,1072,384]{2,1,0:T(8,128)(2,1)S(1)}, f32[3,2080,128]{2,1,0:T(8,128)S(1)}, f32[3,2080,128]{2,1,0:T(8,128)S(...) custom-call(bf16[1920,256]{1,0:T(8,128)(2,1)S(1)} %get-tuple-element, ...), custom_call_target="tpu_custom_call", output_to_operand_aliasing={{0}: (6, {}), {1}: (7, {}), {2}: (8, {}), {3}: (9, {}), {4}... | custom-call | tf_op jit(solution)/shard_map/ends/pallas_call | solution.py:625
  14.0 3.1 %collective-permute-start.2 = (f32[5,1,1536]{2,1,0:T(1,128)S(1)}, f32[5,1,1536]{2,1,0:T(1,128)S(1)}, u32[]{:S(2)}, u32[]{:S(2)}) collective-permute-start(f32[5,1,1536]{2,1,0:T(1,128)S(1)} %get-tuple-element.50), channel_id=1, source_target_pairs={{1,66},{2,65},{3,68},{4,67},{5,70},{6,69},{7,72},{8,71},{9,74},{10... | collective-permute-start | bytes 92168 | tf_op jit(solution)/shard_map/ppermute | solution.py:639
  17.1 0.8 %pick.1 = (f32[3,1,1536]{2,1,0:T(1,128)S(1)}, f32[4,1,1536]{2,1,0:T(1,128)S(1)}) custom-call(bf16[256,256]{1,0:T(8,128)(2,1)S(1)} %get-tuple-element.51.table, s32[3,1,1536]{2,1,0:T(1,128)S(1)} %bitcast.3, f32[8,128]{1,0:T(8,128)S(1)} %get-tuple-element.52.stiffest), custom_call_target="tpu_custom_call" | custom-call | flops 1 | bytes 1 | tf_op jit(solution)/shard_map/pick/pallas_call | solution.py:644
  17.9 0.1 collective-permute-start.4
  18.0 1.7 %collective-permute-start.3 = (f32[3,1,1536]{2,1,0:T(1,128)S(1)}, f32[3,1,1536]{2,1,0:T(1,128)S(1)}, u32[]{:S(2)}, u32[]{:S(2)}) collective-permute-start(f32[3,1,1536]{2,1,0:T(1,128)S(1)} %get-tuple-element.53), channel_id=1, source_target_pairs={{0,64},{1,65},{2,66},{3,67},{4,68},{5,69},{6,70},{7,71},{8,72},{9,... | collective-permute-start | bytes 55304 | tf_op jit(solution)/shard_map/ppermute | solution.py:639
  19.7 2.2 %own.1 = f32[2048,128]{1,0:T(8,128)S(1)} custom-call(s32[3,1,1536]{2,1,0:T(1,128)S(1)} %bitcast.4, f32[3,1,1536]{2,1,0:T(1,128)S(1)} %bitcast.7, f32[2080,128]{1,0:T(8,128)S(1)} %get-tuple-element.57.compact), custom_call_target="tpu_custom_call" | custom-call | tf_op jit(solution)/shard_map/own/pallas_call | solution.py:655
  21.9 0.0 collective-permute-done.3.got_mid
  21.9 0.0 collective-permute-done.4.got_near
  21.9 1.3 %half_couple.1 = (f32[128,256]{1,0:T(8,128)S(1)}, f32[8,128]{1,0:T(8,128)S(1)}) custom-call(f32[3,1,1536]{2,1,0:T(1,128)S(1)} %collective-permute-done.3.got_mid, f32[4,1,1536]{2,1,0:T(1,128)S(1)} %collective-permute-done.4.got_near, s32[3,1,1536]{2,1,0:T(1,128)S(1)} %bitcast.5, f32[3,1,1536]{2,1,0:T(1,128)S(1)} %bitcast.8, ...), custom_call_target="tpu_custom_call" | custom-call | flops 1 | bytes 1 | tf_op jit(solution)/shard_map/half_couple/pallas_call | solution.py:664
  23.2 0.0 collective-permute-done.2.got_far
  23.2 1.0 %couple.1 = (f32[2080,128]{1,0:T(8,128)S(1)}, f32[64,1,128]{2,1,0:T(1,128)S(1)}) custom-call(f32[5,1,1536]{2,1,0:T(1,128)S(1)} %collective-permute-done.2.got_far, s32[3,1,1536]{2,1,0:T(1,128)S(1)} %bitcast.6, f32[3,1,1536]{2,1,0:T(1,128)S(1)} %bitcast.9, f32[128,256]{1,0:T(8,128)S(1)} %get-tuple-element.55.partial, f32[8,128]{1,0:T(8,128)S(1)} %get-tuple-element.56.most, ...), custom_call_target="tpu_custom_call" | custom-call | tf_op jit(solution)/shard_map/couple/pallas_call | solution.py:673
  24.2 22.2 %all_to_all.5.parcel = f32[64,1,128]{2,1,0:T(1,128)S(1)} all-to-all(f32[64,1,128]{2,1,0:T(1,128)S(1)} %get-tuple-element.58), channel_id=1, replica_groups=mesh['grp'=2,'patch'=64] {'patch'}, dimensions={0} | all-to-all | bytes 65536 | tf_op jit(solution)/shard_map/all_to_all | solution.py:682
  46.4 14.3 %steps.1 = (f32[1,2048,384]{2,1,0:T(8,128)}, f32[1,2048,384]{2,1,0:T(8,128)}, f32[2080,128]{1,0:T(8,128)S(1)}) custom-call(f32[64,1,128]{2,1,0:T(1,128)S(1)} %all_to_all.5.parcel, f32[3,2080,128]{2,1,0:T(8,128)S(1)} %get-tuple-element.59.field, f32[3,2080,128]{2,1,0:T(8,128)S(1)} %get-tuple-element.60.moving, ...), custom_call_target="tpu_custom_call", output_to_operand_aliasing={{2}: (7, {})} | custom-call | tf_op jit(solution)/shard_map/steps/pallas_call | solution.py:684
  (12 shorter events, 0.0 us)
Async XLA Ops:
  0.6 5.1 %copy-start.2 = (f32[1,2048,384]{2,1,0:T(8,128)S(1)}, f32[1,2048,384]{2,1,0:T(8,128)}, u32[]{:S(2)}) copy-start(f32[1,2048,384]{2,1,0:T(8,128)} %displace.3) | copy-start | bytes 9437188
  0.6 5.1 %copy-start.5 = (bf16[5,384,384]{2,1,0:T(8,128)(2,1)S(1)}, bf16[5,384,384]{2,1,0:T(8,128)(2,1)}, u32[]{:S(2)}) copy-start(bf16[5,384,384]{2,1,0:T(8,128)(2,1)} %stiff.1) | copy-start | bytes 4423684
  0.7 6.4 %copy-start.1 = (f32[1,2048,384]{2,1,0:T(8,128)S(1)}, f32[1,2048,384]{2,1,0:T(8,128)}, u32[]{:S(2)}) copy-start(f32[1,2048,384]{2,1,0:T(8,128)} %ext_force.3) | copy-start | bytes 9437188
  0.7 6.4 %copy-start.4 = (f32[1,2048,128]{2,1,0:T(8,128)S(1)}, f32[1,2048,128]{2,1,0:T(8,128)}, u32[]{:S(2)}) copy-start(f32[1,2048,128]{2,1,0:T(8,128)} %thickness.3) | copy-start | bytes 3145732
  1.7 5.3 %copy-start = (f32[1,2048,384]{2,1,0:T(8,128)S(1)}, f32[1,2048,384]{2,1,0:T(8,128)}, u32[]{:S(2)}) copy-start(f32[1,2048,384]{2,1,0:T(8,128)} %velocity.3) | copy-start | bytes 9437188
  1.7 5.3 %copy-start.3 = (f32[1,2048,128]{2,1,0:T(8,128)S(1)}, f32[1,2048,128]{2,1,0:T(8,128)}, u32[]{:S(2)}) copy-start(f32[1,2048,128]{2,1,0:T(8,128)} %inv_mass.3) | copy-start | bytes 3145732
  1.7 10.7 %collective-permute-start.1 = (f32[8,1408]{1,0:T(8,128)S(1)}, f32[8,1408]{1,0:T(8,128)S(1)}, u32[]{:S(2)}, u32[]{:S(2)}) collective-permute-start(f32[8,1408]{1,0:T(8,128)S(1)} %get-tuple-element.40), channel_id=1, source_target_pairs={{1,2},{2,1},{3,4},{4,3},{5,6},{6,5},{7,8},{8,7},{9,10},{10,9},{11,... | collective-permute-start | bytes 135176 | tf_op jit(solution)/shard_map/ppermute | solution.py:597
  6.9 5.5 %collective-permute-start = (f32[8,1408]{1,0:T(8,128)S(1)}, f32[8,1408]{1,0:T(8,128)S(1)}, u32[]{:S(2)}, u32[]{:S(2)}) collective-permute-start(f32[8,1408]{1,0:T(8,128)S(1)} %get-tuple-element.39), channel_id=1, source_target_pairs={{0,1},{1,0},{2,3},{3,2},{4,5},{5,4},{6,7},{7,6},{8,9},{9,8},{10,11... | collective-permute-start | bytes 135176 | tf_op jit(solution)/shard_map/ppermute | solution.py:609
  7.1 5.4 %copy-start.6 = (s32[1,1,3,1536]{3,1,2,0:T(1,128)S(1)}, s32[1,1,3,1536]{3,1,2,0:T(1,128)}, u32[]{:S(2)}) copy-start(s32[1,1,3,1536]{3,1,2,0:T(1,128)} %param.14) | copy-start | bytes 55300
  12.4 7.3 %copy-start.7 = (f32[1,1,3,1536]{3,1,2,0:T(1,128)S(1)}, f32[1,1,3,1536]{3,1,2,0:T(1,128)}, u32[]{:S(2)}) copy-start(f32[1,1,3,1536]{3,1,2,0:T(1,128)} %param.15) | copy-start | bytes 55300
  14.0 9.2 %collective-permute-start.2 = (f32[5,1,1536]{2,1,0:T(1,128)S(1)}, f32[5,1,1536]{2,1,0:T(1,128)S(1)}, u32[]{:S(2)}, u32[]{:S(2)}) collective-permute-start(f32[5,1,1536]{2,1,0:T(1,128)S(1)} %get-tuple-element.50), channel_id=1, source_target_pairs={{1,66},{2,65},{3,68},{4,67},{5,70},{6,69},{7,72},{8,71},{9,74},{10... | collective-permute-start | bytes 92168 | tf_op jit(solution)/shard_map/ppermute | solution.py:639
  17.9 4.0 %collective-permute-start.4 = (f32[4,1,1536]{2,1,0:T(1,128)S(1)}, f32[4,1,1536]{2,1,0:T(1,128)S(1)}, u32[]{:S(2)}, u32[]{:S(2)}) collective-permute-start(f32[4,1,1536]{2,1,0:T(1,128)S(1)} %get-tuple-element.54), channel_id=1, source_target_pairs={{0,65},{1,64},{2,67},{3,66},{4,69},{5,68},{6,71},{7,70},{8,73},{9,... | collective-permute-start | bytes 73736 | tf_op jit(solution)/shard_map/ppermute | solution.py:639
  18.0 3.9 %collective-permute-start.3 = (f32[3,1,1536]{2,1,0:T(1,128)S(1)}, f32[3,1,1536]{2,1,0:T(1,128)S(1)}, u32[]{:S(2)}, u32[]{:S(2)}) collective-permute-start(f32[3,1,1536]{2,1,0:T(1,128)S(1)} %get-tuple-element.53), channel_id=1, source_target_pairs={{0,64},{1,65},{2,66},{3,67},{4,68},{5,69},{6,70},{7,71},{8,72},{9,... | collective-permute-start | bytes 55304 | tf_op jit(solution)/shard_map/ppermute | solution.py:639
